TPU v7x, 256 devices: a whole 4x4x8 slice. The times are simulated.
256 devices in a mesh: gx: 16 (over y_lo, z), gy: 16 (over y_hi, x, core).
Axes of the slice: x: 4, y: 4 (y_hi: 2, y_lo: 2; y = y_hi * 2 + y_lo), z: 8, core: 2. Of those that a mesh axis runs over, the one named last changes fastest.
Arguments:
- right_side: float32 [3, 64, 128, 2048], P(None, None, 'gx', 'gy'), may hold values from -8 to 8
- material: int32 [64, 128, 2048], P(None, 'gx', 'gy'), may hold values from 0 to 15
- conductivity: float32 [16], replicated, may hold values from 0.1 to 10
Outputs:
- corrected: float32 [3, 64, 128, 2048], P(None, None, 'gx', 'gy')
- final_residual: float32 [3, 64, 128, 2048], P(None, None, 'gx', 'gy')
Inputs may be any that keep to these rules, and one draw needn't show every extreme that they name: material class of each cell, an index into conductivity.
All inputs are finite; a program needn't handle non-finite values.
Results may differ from a plain program's by a relative error of at most 0.00002.
Values sent between devices are 32-bit elements; how exact they have to be, the bound alone decides.
A program may use at most 64 MiB of HBM per device.

v0:
```python
import jax
import jax.numpy as jnp
from jax import lax
from jax.sharding import PartitionSpec as P

OMEGA_EDGE = 0.6
OMEGA_NODE = 0.7
OMEGA_VECTOR = 0.5
across_z = 0
across_x = 1
across_y = 2


def padded(array, sides, width):
    for axis, dim in sides:
        count, length = (lax.axis_size(axis), array.shape[dim])
        up = [(i, (i + 1) % count) for i in range(count - 1)]
        down = [(j, i) for i, j in up]
        last = lax.slice_in_dim(array, length - width, length, axis=dim)
        leading = lax.slice_in_dim(array, 0, width, axis=dim)
        before = lax.ppermute(last, axis, up)
        after = lax.ppermute(leading, axis, down)
        array = jnp.concatenate([before, array, after], axis=dim)
    return array


def from_behind(block, axis, distance):
    devices = range(lax.axis_size(axis))
    route = [(i - distance, i) for i in devices if i - distance in devices]
    return lax.ppermute(block, axis, route)


def forward(values, dimension):
    count = values.shape[dimension]
    widths = [(0, 0)] * values.ndim
    widths[dimension] = (0, 1)
    return lax.slice_in_dim(jnp.pad(values, widths), 1, count + 1, axis=dimension)


def backward(values, dimension):
    count = values.shape[dimension]
    widths = [(0, 0)] * values.ndim
    widths[dimension] = (1, 0)
    return lax.slice_in_dim(jnp.pad(values, widths), 0, count, axis=dimension)


def curl_faces(edge_x, edge_y, edge_z):
    face_z = edge_x - forward(edge_x, across_y) + forward(edge_y, across_x) - edge_y
    face_x = edge_y - forward(edge_y, across_z) + forward(edge_z, across_y) - edge_z
    face_y = edge_z - forward(edge_z, across_x) + forward(edge_x, across_z) - edge_x
    return (face_x, face_y, face_z)


def curl_edges(face_x, face_y, face_z):
    edge_x = face_z - backward(face_z, across_y) - face_y + backward(face_y, across_z)
    edge_y = backward(face_z, across_x) - face_z + face_x - backward(face_x, across_z)
    edge_z = backward(face_x, across_y) - face_x + face_y - backward(face_y, across_x)
    return jnp.stack([edge_x, edge_y, edge_z])


def apply_wide(field, sigma_wide, mask_rows, mask_cols):
    inside = mask_rows[None, :, None] * mask_cols[None, None, :]
    face_x, face_y, face_z = curl_faces(field[0], field[1], field[2])
    return curl_edges(face_x * inside, face_y * inside, face_z * inside) + sigma_wide[None] * field


def prior_x(values, border):
    return jnp.concatenate([border[:, None, :], values[:, :-1, :]], 1)


def prior_y(values, border):
    return jnp.concatenate([border[:, :, None], values[:, :, :-1]], 2)


def later_x(values, border):
    return jnp.concatenate([values[:, 1:, :], border[:, None, :]], 1)


def later_y(values, border):
    return jnp.concatenate([values[:, :, 1:], border[:, :, None]], 2)


def extend_block(stacked, margin):
    return padded(stacked, (("gx", 2), ("gy", 3)), margin)


def local(right_side, material, conductivity):
    depth, cells_x, cells_y = material.shape
    sigma_cell = jnp.zeros(material.shape, jnp.float32)
    for category in range(conductivity.shape[0]):
        sigma_cell = jnp.where(material == category, conductivity[category], sigma_cell)
    margin = 2
    stacked = jnp.concatenate([right_side, sigma_cell[None]], 0)
    extended = extend_block(stacked, margin)
    source_wide = extended[:3]
    sigma_wide = extended[3]
    position_x = (
        lax.axis_index("gx") * cells_x - margin + jnp.arange(cells_x + 2 * margin, dtype=jnp.int32)
    )
    position_y = (
        lax.axis_index("gy") * cells_y - margin + jnp.arange(cells_y + 2 * margin, dtype=jnp.int32)
    )
    mask_rows = ((position_x >= 0) & (position_x < cells_x * lax.axis_size("gx"))).astype(
        jnp.float32
    )
    mask_cols = ((position_y >= 0) & (position_y < cells_y * lax.axis_size("gy"))).astype(
        jnp.float32
    )
    first_wide = OMEGA_EDGE * source_wide / (4.0 + sigma_wide)[None]
    residual_wide = source_wide - apply_wide(first_wide, sigma_wide, mask_rows, mask_cols)
    first = first_wide[:, :, margin : margin + cells_x, margin : margin + cells_y]
    residual = residual_wide[:, :, margin : margin + cells_x, margin : margin + cells_y]
    below_x = residual_wide[0, :, margin - 1, margin : margin + cells_y] * mask_rows[margin - 1]
    below_y = residual_wide[1, :, margin : margin + cells_x, margin - 1] * mask_cols[margin - 1]
    sigma_below_x = sigma_wide[:, margin - 1, margin : margin + cells_y]
    sigma_below_y = sigma_wide[:, margin : margin + cells_x, margin - 1]
    diagonal = 4.0 + sigma_cell
    diag_below_x = (4.0 + sigma_below_x) * mask_rows[margin - 1]
    diag_below_y = (4.0 + sigma_below_y) * mask_cols[margin - 1]
    resid_x = residual[0]
    resid_y = residual[1]
    resid_z = residual[2]
    node_rhs = (
        prior_x(resid_x, below_x)
        - resid_x
        + prior_y(resid_y, below_y)
        - resid_y
        + backward(resid_z, across_z)
        - resid_z
    )
    sigma_prior_x = prior_x(sigma_cell, sigma_below_x)
    sigma_prior_y = prior_y(sigma_cell, sigma_below_y)
    node_diag = 3.0 * sigma_cell + sigma_prior_x + sigma_prior_y + backward(sigma_cell, across_z)
    phi_first = OMEGA_NODE * node_rhs / node_diag
    phi_wide = padded(phi_first, (("gx", 1), ("gy", 2)), 1)
    centre = phi_wide[:, 1:-1, 1:-1]
    right = phi_wide[:, 2:, 1:-1]
    left = phi_wide[:, :-2, 1:-1]
    above = phi_wide[:, 1:-1, 2:]
    below = phi_wide[:, 1:-1, :-2]
    flux_depth = sigma_cell * (forward(centre, across_z) - centre)
    applied = sigma_prior_x * (centre - left) - sigma_cell * (right - centre)
    applied = applied + sigma_prior_y * (centre - below) - sigma_cell * (above - centre)
    applied = applied + backward(flux_depth, across_z) - flux_depth
    phi_second = phi_first + OMEGA_NODE * (node_rhs - applied) / node_diag
    psi_x = (
        OMEGA_VECTOR
        * ((resid_x + prior_x(resid_x, below_x)) / 2.0)
        / ((diagonal + prior_x(diagonal, diag_below_x)) / 4.0)
    )
    psi_y = (
        OMEGA_VECTOR
        * ((resid_y + prior_y(resid_y, below_y)) / 2.0)
        / ((diagonal + prior_y(diagonal, diag_below_y)) / 4.0)
    )
    psi_z = (
        OMEGA_VECTOR
        * ((resid_z + backward(resid_z, across_z)) / 2.0)
        / ((diagonal + backward(diagonal, across_z)) / 4.0)
    )
    after_x = from_behind(jnp.stack([phi_second[:, 0, :], psi_x[:, 0, :]]), "gx", -1)
    after_y = from_behind(jnp.stack([phi_second[:, :, 0], psi_y[:, :, 0]]), "gy", -1)
    part_x = (
        later_x(phi_second, after_x[0]) - phi_second + (psi_x + later_x(psi_x, after_x[1])) / 2.0
    )
    part_y = (
        later_y(phi_second, after_y[0]) - phi_second + (psi_y + later_y(psi_y, after_y[1])) / 2.0
    )
    part_z = forward(phi_second, across_z) - phi_second + (psi_z + forward(psi_z, across_z)) / 2.0
    corrected = first + jnp.stack([part_x, part_y, part_z])
    final_wide = padded(corrected, (("gx", 2), ("gy", 3)), 1)
    sigma_one = sigma_wide[:, margin - 1 : margin + cells_x + 1, margin - 1 : margin + cells_y + 1]
    rows_one = mask_rows[margin - 1 : margin + cells_x + 1]
    cols_one = mask_cols[margin - 1 : margin + cells_y + 1]
    applied_final = apply_wide(final_wide, sigma_one, rows_one, cols_one)[:, :, 1:-1, 1:-1]
    final_residual = right_side - applied_final
    return (corrected, final_residual)


def solution(mesh):
    return jax.shard_map(
        local,
        mesh=mesh,
        in_specs=(P(None, None, "gx", "gy"), P(None, "gx", "gy"), P()),
        out_specs=(P(None, None, "gx", "gy"), P(None, None, "gx", "gy")),
        check_vma=False,
    )
```

profile of v0, /device:TPU:24, one launch (start us, length us, event | category | flops | bytes accessed | tf_op | source)
XLA Modules:
  0.0 132.6 jit_solution(6895135253645581806)
XLA Ops:
  0.6 1.9 %fusion.86 = (f32[1]{0:T(128)}, f32[1]{0:T(128)}, f32[1]{0:T(128)}, f32[1]{0:T(128)}, f32[1]{0:T(128)}, /*index=5*/f32[1]{0:T(128)}, f32[1]{0:T(128)}, f32[1]{0:...) fusion(f32[16]{0:T(128)} %param.5), kind=kLoop, calls=%fused_computation.173 | loop fusion | bytes 128 | tf_op jit(solution)/shard_map/slice | solution.py:91
  3.8 11.2 %broadcast_add_fusion = (f32[64,8,128]{2,0,1:T(8,128)S(1)}, f32[64,8,128]{2,0,1:T(8,128)S(1)}) fusion(f32[]{:T(128)} %bitcast.15, f32[]{:T(128)} %bitcast.14, f32[]{:T(128)} %bitcast.13, f32[]{:T(128)} %bitcast.12, f32[]{:T(128)} %bitcast.11, f32[]{:T(128)} %bitcast.10, f32[]{:T(128)} %bitcast.9, f32[]{:T(128)} %bitcast.8, f32[]{:T(128)} %bitcast.7, ...), kind=kLoop, calls=%fused_computation.152 | loop fusion | flops 2162688 | bytes 786496 | tf_op jit(solution)/shard_map/add | solution.py:117
  15.1 3.8 %collective-permute-start = (f32[4,64,2,128]{3,1,2,0:T(8,128)S(1)}, f32[4,64,2,128]{3,1,2,0:T(8,128)S(1)}, u32[]{:S(2)}, u32[]{:S(2)}) collective-permute-start(f32[4,64,2,128]{3,1,2,0:T(8,128)S(1)} %get-tuple-element.30), channel_id=1, source_target_pairs={{0,16},{16,32},{32,48},{48,64},{64,80},{80,96},{96,112},{112,128},... | collective-permute-start | bytes 786440 | tf_op jit(solution)/shard_map/ppermute | solution.py:21
  18.9 6.0 %collective-permute-start.1 = (f32[4,64,2,128]{3,1,2,0:T(8,128)S(1)}, f32[4,64,2,128]{3,1,2,0:T(8,128)S(1)}, u32[]{:S(2)}, u32[]{:S(2)}) collective-permute-start(f32[4,64,2,128]{3,1,2,0:T(8,128)S(1)} %get-tuple-element.31), channel_id=1, source_target_pairs={{16,0},{32,16},{48,32},{64,48},{80,64},{96,80},{112,96},{128,112},... | collective-permute-start | bytes 786440 | tf_op jit(solution)/shard_map/ppermute | solution.py:22
  25.0 4.3 %collective-permute-done = f32[4,64,2,128]{3,1,2,0:T(8,128)S(1)} collective-permute-done((f32[4,64,2,128]{3,1,2,0:T(8,128)S(1)}, f32[4,64,2,128]{3,1,2,0:T(8,128)S(1)}, u32[]{:S(2)}, u32[]{:S(2)}) %collective-permute-start) | collective-permute-done | bytes 262176 | tf_op jit(solution)/shard_map/ppermute | solution.py:21
  30.6 1.7 %fusion.81 = (f32[4,64,12,2]{3,1,2,0:T(8,128)}, f32[4,64,12,2]{3,1,2,0:T(8,128)S(1)}) fusion(f32[4,64,12,128]{3,1,2,0:T(8,128)S(1)} %pad_maximum_fusion.2), kind=kLoop, calls=%fused_computation.168 | loop fusion | bytes 98304 | tf_op jit(solution)/shard_map/slice | solution.py:19
  32.3 1.9 %copy.164 = f32[4,64,12,2]{1,0,3,2:T(4,128)S(1)} copy(f32[4,64,12,2]{3,1,2,0:T(8,128)} %get-tuple-element.28) | data formatting | bytes 49152 | tf_op jit(solution)/shard_map/slice | solution.py:19
  34.3 1.9 %collective-permute-start.2 = (f32[4,64,12,2]{1,0,3,2:T(4,128)S(1)}, f32[4,64,12,2]{1,0,3,2:T(4,128)S(1)}, u32[]{:S(2)}, u32[]{:S(2)}) collective-permute-start(f32[4,64,12,2]{1,0,3,2:T(4,128)S(1)} %copy.164), channel_id=1, source_target_pairs={{0,1},{1,2},{2,3},{3,4},{4,5},{5,6},{6,7},{7,8},{8,9},{9,10},{10,1... | collective-permute-start | bytes 73736 | tf_op jit(solution)/shard_map/ppermute | solution.py:21
  37.3 7.2 %collective-permute-start.3 = (f32[4,64,12,2]{1,0,3,2:T(4,128)}, f32[4,64,12,2]{1,0,3,2:T(4,128)}, u32[]{:S(2)}, u32[]{:S(2)}) collective-permute-start(f32[4,64,12,2]{1,0,3,2:T(4,128)} %copy.165), channel_id=1, source_target_pairs={{1,0},{2,1},{3,2},{4,3},{5,4},{6,5},{7,6},{8,7},{9,8},{10,9},{11,1... | collective-permute-start | bytes 73736 | tf_op jit(solution)/shard_map/ppermute | solution.py:22
  47.9 2.5 %copy.167 = f32[4,64,12,2]{3,1,2,0:T(8,128)} copy(f32[4,64,12,2]{1,0,3,2:T(4,128)} %collective-permute-done.3) | data formatting | bytes 49152 | tf_op jit(solution)/shard_map/ppermute | solution.py:22
  50.4 1.5 %add_bitcast_fusion = (f32[64,12,132]{2,0,1:T(8,128)S(1)}, f32[1,64,12,132]{3,1,2,0:T(8,128)S(1)}) fusion(f32[4,64,12,2]{3,1,2,0:T(8,128)} %copy.167, f32[4,64,2,128]{3,1,2,0:T(8,128)S(1)} %collective-permute-done.1, f32[1,64,8,128]{3,1,2,0:T(8,128)S(1)} %bitcast.91, f32[3,64,8,128]{3,1,2,0:T(8,128)S(1)} %copy.163, ...), kind=kLoop, calls=%fused_computation.44 | loop fusion | flops 608256 | bytes 2433024 | tf_op jit(solution)/shard_map/div | solution.py:109
  60.5 2.1 %collective-permute-start.4 = (f32[64,1,128]{2,0,1:T(8,128)S(1)}, f32[64,1,128]{2,0,1:T(8,128)S(1)}, u32[]{:S(2)}, u32[]{:S(2)}) collective-permute-start(f32[64,1,128]{2,0,1:T(8,128)S(1)} %get-tuple-element.59), channel_id=1, source_target_pairs={{0,16},{16,32},{32,48},{48,64},{64,80},{80,96},{96,112},{112,128},... | collective-permute-start | bytes 98312 | tf_op jit(solution)/shard_map/ppermute | solution.py:21
  62.6 6.3 %collective-permute-start.5 = (f32[64,1,128]{2,0,1:T(8,128)S(1)}, f32[64,1,128]{2,0,1:T(8,128)S(1)}, u32[]{:S(2)}, u32[]{:S(2)}) collective-permute-start(f32[64,1,128]{2,0,1:T(8,128)S(1)} %get-tuple-element.60), channel_id=1, source_target_pairs={{16,0},{32,16},{48,32},{64,48},{80,64},{96,80},{112,96},{128,112},... | collective-permute-start | bytes 98312 | tf_op jit(solution)/shard_map/ppermute | solution.py:22
  70.7 1.9 %collective-permute-start.6 = (f32[64,10,1]{2,0,1:T(8,128)S(1)}, f32[64,10,1]{2,0,1:T(8,128)S(1)}, u32[]{:S(2)}, u32[]{:S(2)}) collective-permute-start(f32[64,10,1]{2,0,1:T(8,128)S(1)} %get-tuple-element.52), channel_id=1, source_target_pairs={{0,1},{1,2},{2,3},{3,4},{4,5},{5,6},{6,7},{7,8},{8,9},{9,10},{10,1... | collective-permute-start | bytes 7688 | tf_op jit(solution)/shard_map/ppermute | solution.py:21
  72.6 7.3 %collective-permute-start.7 = (f32[64,10,1]{2,0,1:T(8,128)S(1)}, f32[64,10,1]{2,0,1:T(8,128)S(1)}, u32[]{:S(2)}, u32[]{:S(2)}) collective-permute-start(f32[64,10,1]{2,0,1:T(8,128)S(1)} %get-tuple-element.53), channel_id=1, source_target_pairs={{1,0},{2,1},{3,2},{4,3},{5,4},{6,5},{7,6},{8,7},{9,8},{10,9},{11,1... | collective-permute-start | bytes 7688 | tf_op jit(solution)/shard_map/ppermute | solution.py:22
  82.7 1.8 %collective-permute-done.7 = f32[64,10,1]{2,0,1:T(8,128)S(1)} collective-permute-done((f32[64,10,1]{2,0,1:T(8,128)S(1)}, f32[64,10,1]{2,0,1:T(8,128)S(1)}, u32[]{:S(2)}, u32[]{:S(2)}) %collective-permute-start.7) | collective-permute-done | bytes 2592 | tf_op jit(solution)/shard_map/ppermute | solution.py:22
  85.1 7.4 %collective-permute-start.9 = (f32[2,64,8]{1,2,0:T(8,128)S(1)}, f32[2,64,8]{1,2,0:T(8,128)S(1)}, u32[]{:S(2)}, u32[]{:S(2)}) collective-permute-start(f32[2,64,8]{1,2,0:T(8,128)S(1)} %pad_maximum_fusion.23), channel_id=1, source_target_pairs={{1,0},{2,1},{3,2},{4,3},{5,4},{6,5},{7,6},{8,7},{9,8},{10,9},{11,1... | collective-permute-start | bytes 12296 | tf_op jit(solution)/shard_map/ppermute | solution.py:30
  93.4 6.3 %collective-permute-start.8 = (f32[2,64,128]{2,1,0:T(8,128)S(1)}, f32[2,64,128]{2,1,0:T(8,128)S(1)}, u32[]{:S(2)}, u32[]{:S(2)}) collective-permute-start(f32[2,64,128]{2,1,0:T(8,128)S(1)} %pad_maximum_fusion.22), channel_id=1, source_target_pairs={{16,0},{32,16},{48,32},{64,48},{80,64},{96,80},{112,96},{128,112},... | collective-permute-start | bytes 196616 | tf_op jit(solution)/shard_map/ppermute | solution.py:30
  101.6 1.8 %fusion.73 = (f32[1,64,8,128]{3,1,2,0:T(8,128)S(1)}, f32[1,64,8,128]{3,1,2,0:T(8,128)S(1)}, f32[1,64,8,128]{3,1,2,0:T(8,128)S(1)}) fusion(f32[64,8,128]{2,0,1:T(8,128)S(1)} %fusion.49, f32[64,1,128]{2,0,1:T(8,128)S(1)} %get-tuple-element.62, f32[64,7,128]{2,0,1:T(8,128)} %slice.447, f32[64,8,128]{2,0,1:T(8,128)S(1)} %get-tuple-element.57, ...), kind=kLoop, calls=%fused_computation.137 | loop fusion | flops 1048576 | bytes 2883584 | tf_op jit(solution)/shard_map/stack | solution.py:170
  103.7 1.9 %collective-permute-start.10 = (f32[3,64,1,128]{3,1,2,0:T(8,128)S(1)}, f32[3,64,1,128]{3,1,2,0:T(8,128)S(1)}, u32[]{:S(2)}, u32[]{:S(2)}) collective-permute-start(f32[3,64,1,128]{3,1,2,0:T(8,128)S(1)} %get-tuple-element.37), channel_id=1, source_target_pairs={{0,16},{16,32},{32,48},{48,64},{64,80},{80,96},{96,112},{112,128},... | collective-permute-start | bytes 294920 | tf_op jit(solution)/shard_map/ppermute | solution.py:21
  105.7 6.4 %collective-permute-start.11 = (f32[3,64,1,128]{3,1,2,0:T(8,128)S(1)}, f32[3,64,1,128]{3,1,2,0:T(8,128)S(1)}, u32[]{:S(2)}, u32[]{:S(2)}) collective-permute-start(f32[3,64,1,128]{3,1,2,0:T(8,128)S(1)} %get-tuple-element.38), channel_id=1, source_target_pairs={{16,0},{32,16},{48,32},{64,48},{80,64},{96,80},{112,96},{128,112},... | collective-permute-start | bytes 294920 | tf_op jit(solution)/shard_map/ppermute | solution.py:22
  112.7 1.5 %collective-permute-done.11 = f32[3,64,1,128]{3,1,2,0:T(8,128)S(1)} collective-permute-done((f32[3,64,1,128]{3,1,2,0:T(8,128)S(1)}, f32[3,64,1,128]{3,1,2,0:T(8,128)S(1)}, u32[]{:S(2)}, u32[]{:S(2)}) %collective-permute-start.11) | collective-permute-done | bytes 98336 | tf_op jit(solution)/shard_map/ppermute | solution.py:22
  115.0 1.9 %collective-permute-start.12 = (f32[3,64,10,1]{1,3,2,0:T(1,128)S(1)}, f32[3,64,10,1]{1,3,2,0:T(1,128)S(1)}, u32[]{:S(2)}, u32[]{:S(2)}) collective-permute-start(f32[3,64,10,1]{1,3,2,0:T(1,128)S(1)} %copy.171), channel_id=1, source_target_pairs={{0,1},{1,2},{2,3},{3,4},{4,5},{5,6},{6,7},{7,8},{8,9},{9,10},{10,1... | collective-permute-start | bytes 23048 | tf_op jit(solution)/shard_map/ppermute | solution.py:21
  117.3 7.4 %collective-permute-start.13 = (f32[3,64,10,1]{1,3,2,0:T(1,128)S(1)}, f32[3,64,10,1]{1,3,2,0:T(1,128)S(1)}, u32[]{:S(2)}, u32[]{:S(2)}) collective-permute-start(f32[3,64,10,1]{1,3,2,0:T(1,128)S(1)} %copy.172), channel_id=1, source_target_pairs={{1,0},{2,1},{3,2},{4,3},{5,4},{6,5},{7,6},{8,7},{9,8},{10,9},{11,1... | collective-permute-start | bytes 23048 | tf_op jit(solution)/shard_map/ppermute | solution.py:22
  (85 shorter events, 33.3 us)
Async XLA Ops:
  15.1 14.2 %collective-permute-start = (f32[4,64,2,128]{3,1,2,0:T(8,128)S(1)}, f32[4,64,2,128]{3,1,2,0:T(8,128)S(1)}, u32[]{:S(2)}, u32[]{:S(2)}) collective-permute-start(f32[4,64,2,128]{3,1,2,0:T(8,128)S(1)} %get-tuple-element.30), channel_id=1, source_target_pairs={{0,16},{16,32},{32,48},{48,64},{64,80},{80,96},{96,112},{112,128},... | collective-permute-start | bytes 786440 | tf_op jit(solution)/shard_map/ppermute | solution.py:21
  18.9 11.6 %collective-permute-start.1 = (f32[4,64,2,128]{3,1,2,0:T(8,128)S(1)}, f32[4,64,2,128]{3,1,2,0:T(8,128)S(1)}, u32[]{:S(2)}, u32[]{:S(2)}) collective-permute-start(f32[4,64,2,128]{3,1,2,0:T(8,128)S(1)} %get-tuple-element.31), channel_id=1, source_target_pairs={{16,0},{32,16},{48,32},{64,48},{80,64},{96,80},{112,96},{128,112},... | collective-permute-start | bytes 786440 | tf_op jit(solution)/shard_map/ppermute | solution.py:22
  34.3 13.1 %collective-permute-start.2 = (f32[4,64,12,2]{1,0,3,2:T(4,128)S(1)}, f32[4,64,12,2]{1,0,3,2:T(4,128)S(1)}, u32[]{:S(2)}, u32[]{:S(2)}) collective-permute-start(f32[4,64,12,2]{1,0,3,2:T(4,128)S(1)} %copy.164), channel_id=1, source_target_pairs={{0,1},{1,2},{2,3},{3,4},{4,5},{5,6},{6,7},{7,8},{8,9},{9,10},{10,1... | collective-permute-start | bytes 73736 | tf_op jit(solution)/shard_map/ppermute | solution.py:21
  37.3 10.6 %collective-permute-start.3 = (f32[4,64,12,2]{1,0,3,2:T(4,128)}, f32[4,64,12,2]{1,0,3,2:T(4,128)}, u32[]{:S(2)}, u32[]{:S(2)}) collective-permute-start(f32[4,64,12,2]{1,0,3,2:T(4,128)} %copy.165), channel_id=1, source_target_pairs={{1,0},{2,1},{3,2},{4,3},{5,4},{6,5},{7,6},{8,7},{9,8},{10,9},{11,1... | collective-permute-start | bytes 73736 | tf_op jit(solution)/shard_map/ppermute | solution.py:22
  50.4 1.5 %copy-start = (f32[4,64,12,2]{3,1,2,0:T(8,128)S(1)}, f32[4,64,12,2]{3,1,2,0:T(8,128)}, u32[]{:S(2)}) copy-start(f32[4,64,12,2]{3,1,2,0:T(8,128)} %copy.167) | copy-start | bytes 73732
  52.0 6.5 %copy-start.1 = (f32[1,64,12,132]{3,1,2,0:T(8,128)}, f32[1,64,12,132]{3,1,2,0:T(8,128)S(1)}, u32[]{:S(2)}) copy-start(f32[1,64,12,132]{3,1,2,0:T(8,128)S(1)} %get-tuple-element.17) | copy-start | bytes 1216516
  55.8 4.2 %copy-start.3 = (f32[64,7,128]{2,0,1:T(8,128)S(1)}, f32[64,7,128]{2,0,1:T(8,128)}, u32[]{:S(2)}) copy-start(f32[64,7,128]{2,0,1:T(8,128)} %slice.440) | copy-start | bytes 688132
  59.2 9.7 %copy-start.4 = (f32[64,7,128]{2,0,1:T(8,128)S(1)}, f32[64,7,128]{2,0,1:T(8,128)}, u32[]{:S(2)}) copy-start(f32[64,7,128]{2,0,1:T(8,128)} %slice.449) | copy-start | bytes 688132
  60.5 8.6 %collective-permute-start.4 = (f32[64,1,128]{2,0,1:T(8,128)S(1)}, f32[64,1,128]{2,0,1:T(8,128)S(1)}, u32[]{:S(2)}, u32[]{:S(2)}) collective-permute-start(f32[64,1,128]{2,0,1:T(8,128)S(1)} %get-tuple-element.59), channel_id=1, source_target_pairs={{0,16},{16,32},{32,48},{48,64},{64,80},{80,96},{96,112},{112,128},... | collective-permute-start | bytes 98312 | tf_op jit(solution)/shard_map/ppermute | solution.py:21
  62.6 7.9 %collective-permute-start.5 = (f32[64,1,128]{2,0,1:T(8,128)S(1)}, f32[64,1,128]{2,0,1:T(8,128)S(1)}, u32[]{:S(2)}, u32[]{:S(2)}) collective-permute-start(f32[64,1,128]{2,0,1:T(8,128)S(1)} %get-tuple-element.60), channel_id=1, source_target_pairs={{16,0},{32,16},{48,32},{64,48},{80,64},{96,80},{112,96},{128,112},... | collective-permute-start | bytes 98312 | tf_op jit(solution)/shard_map/ppermute | solution.py:22
  70.7 12.0 %collective-permute-start.6 = (f32[64,10,1]{2,0,1:T(8,128)S(1)}, f32[64,10,1]{2,0,1:T(8,128)S(1)}, u32[]{:S(2)}, u32[]{:S(2)}) collective-permute-start(f32[64,10,1]{2,0,1:T(8,128)S(1)} %get-tuple-element.52), channel_id=1, source_target_pairs={{0,1},{1,2},{2,3},{3,4},{4,5},{5,6},{6,7},{7,8},{8,9},{9,10},{10,1... | collective-permute-start | bytes 7688 | tf_op jit(solution)/shard_map/ppermute | solution.py:21
  72.6 11.8 %collective-permute-start.7 = (f32[64,10,1]{2,0,1:T(8,128)S(1)}, f32[64,10,1]{2,0,1:T(8,128)S(1)}, u32[]{:S(2)}, u32[]{:S(2)}) collective-permute-start(f32[64,10,1]{2,0,1:T(8,128)S(1)} %get-tuple-element.53), channel_id=1, source_target_pairs={{1,0},{2,1},{3,2},{4,3},{5,4},{6,5},{7,6},{8,7},{9,8},{10,9},{11,1... | collective-permute-start | bytes 7688 | tf_op jit(solution)/shard_map/ppermute | solution.py:22
  85.1 14.6 %collective-permute-start.9 = (f32[2,64,8]{1,2,0:T(8,128)S(1)}, f32[2,64,8]{1,2,0:T(8,128)S(1)}, u32[]{:S(2)}, u32[]{:S(2)}) collective-permute-start(f32[2,64,8]{1,2,0:T(8,128)S(1)} %pad_maximum_fusion.23), channel_id=1, source_target_pairs={{1,0},{2,1},{3,2},{4,3},{5,4},{6,5},{7,6},{8,7},{9,8},{10,9},{11,1... | collective-permute-start | bytes 12296 | tf_op jit(solution)/shard_map/ppermute | solution.py:30
  93.4 8.2 %collective-permute-start.8 = (f32[2,64,128]{2,1,0:T(8,128)S(1)}, f32[2,64,128]{2,1,0:T(8,128)S(1)}, u32[]{:S(2)}, u32[]{:S(2)}) collective-permute-start(f32[2,64,128]{2,1,0:T(8,128)S(1)} %pad_maximum_fusion.22), channel_id=1, source_target_pairs={{16,0},{32,16},{48,32},{64,48},{80,64},{96,80},{112,96},{128,112},... | collective-permute-start | bytes 196616 | tf_op jit(solution)/shard_map/ppermute | solution.py:30
  103.7 9.0 %collective-permute-start.10 = (f32[3,64,1,128]{3,1,2,0:T(8,128)S(1)}, f32[3,64,1,128]{3,1,2,0:T(8,128)S(1)}, u32[]{:S(2)}, u32[]{:S(2)}) collective-permute-start(f32[3,64,1,128]{3,1,2,0:T(8,128)S(1)} %get-tuple-element.37), channel_id=1, source_target_pairs={{0,16},{16,32},{32,48},{48,64},{64,80},{80,96},{96,112},{112,128},... | collective-permute-start | bytes 294920 | tf_op jit(solution)/shard_map/ppermute | solution.py:21
  105.7 8.6 %collective-permute-start.11 = (f32[3,64,1,128]{3,1,2,0:T(8,128)S(1)}, f32[3,64,1,128]{3,1,2,0:T(8,128)S(1)}, u32[]{:S(2)}, u32[]{:S(2)}) collective-permute-start(f32[3,64,1,128]{3,1,2,0:T(8,128)S(1)} %get-tuple-element.38), channel_id=1, source_target_pairs={{16,0},{32,16},{48,32},{64,48},{80,64},{96,80},{112,96},{128,112},... | collective-permute-start | bytes 294920 | tf_op jit(solution)/shard_map/ppermute | solution.py:22
  115.0 12.3 %collective-permute-start.12 = (f32[3,64,10,1]{1,3,2,0:T(1,128)S(1)}, f32[3,64,10,1]{1,3,2,0:T(1,128)S(1)}, u32[]{:S(2)}, u32[]{:S(2)}) collective-permute-start(f32[3,64,10,1]{1,3,2,0:T(1,128)S(1)} %copy.171), channel_id=1, source_target_pairs={{0,1},{1,2},{2,3},{3,4},{4,5},{5,6},{6,7},{7,8},{8,9},{9,10},{10,1... | collective-permute-start | bytes 23048 | tf_op jit(solution)/shard_map/ppermute | solution.py:21
  117.3 10.4 %collective-permute-start.13 = (f32[3,64,10,1]{1,3,2,0:T(1,128)S(1)}, f32[3,64,10,1]{1,3,2,0:T(1,128)S(1)}, u32[]{:S(2)}, u32[]{:S(2)}) collective-permute-start(f32[3,64,10,1]{1,3,2,0:T(1,128)S(1)} %copy.172), channel_id=1, source_target_pairs={{1,0},{2,1},{3,2},{4,3},{5,4},{6,5},{7,6},{8,7},{9,8},{10,9},{11,1... | collective-permute-start | bytes 23048 | tf_op jit(solution)/shard_map/ppermute | solution.py:22
  129.7 1.1 copy-start.2
where the time goes:
time: 134 us; the launch traced here: 133 us
  starting transfers between devices  68 us (51%)
  other arithmetic  26.1 us (19%)
  local copies, waits for them, and re-layouts  25.3 us (19%)
  waiting for transfers between devices  12 us (9%)
    ppermute x6, starting transfers between devices, padded(): after = lax.ppermute(leading, axis, down)  40.7 us
    ppermute x2, starting transfers between devices, from_behind(): return lax.ppermute(block, axis, route)  13.8 us
    ppermute x6, starting transfers between devices, padded(): before = lax.ppermute(last, axis, up)  13.6 us
    add x1, other arithmetic, local(): diagonal = 4.0 + sigma_cell  11.2 us
    ppermute x6, waiting for transfers between devices, padded(): before = lax.ppermute(last, axis, up)  5.96 us
    ppermute x6, waiting for transfers between devices, padded(): after = lax.ppermute(leading, axis, down)  5.87 us
    unnamed x13, local copies, waits for them, and re-layouts  4.58 us
    slice x7, local copies, waits for them, and re-layouts, padded(): last = lax.slice_in_dim(array, length - width, length, axis=dim)  4.55 us
  transfers between devices with their start and end apart: 14, of which 8 were waited for; matrix products, arithmetic and copies ran while one was open for 9% of the time, Pallas kernels for 0%

commit v1 on v0

v1 whole, which is shorter than its diff:
```python
import functools

import jax
import jax.numpy as jnp
from jax import lax
from jax.experimental import pallas as pl
from jax.experimental.pallas import tpu as pltpu
from jax.sharding import PartitionSpec as P

OMEGA_EDGE = 0.6
OMEGA_NODE = 0.7
LANES = 128
TILE = 8
PAD = 8
ROWS = 12
BAND = 12
GROUP = 8
CHUNKS = 4
MESH = pl.DeviceIdType.MESH

NAMES = (
    "fx", "fy", "fz", "tx", "ty", "tz", "sg", "sy", "p1", "nr",
    "rn", "gz", "gx", "rx", "ry", "rz", "sz", "px", "py", "fl",
    "p2", "pz", "qz", "qx", "qy", "gy",
)
PADDED = (
    "fx", "fy", "tz", "sg", "p1", "gy", "gx", "rz", "fl", "p2",
    "sz", "px", "py", "qy", "qx",
)


def roll(value, shift):
    shift = shift % LANES
    return value if shift == 0 else pltpu.roll(value, shift, 1)


def kernel(
    sizes,
    cond,
    rs_hbm,
    rs_flat,
    mat_hbm,
    mat_flat,
    corr_out,
    res_out,
    raw,
    mat,
    halo_rs,
    halo_mat,
    pack,
    pack_recv,
    corner,
    corner_recv,
    band,
    *rest,
):
    bufs = dict(zip(NAMES, rest[: len(NAMES)]))
    in_sem, x_send, x_recv, y_send, y_recv, c_send, c_recv = rest[len(NAMES) :]
    count_x, count_y, depth, rows, cols = sizes
    tiles = depth // TILE
    ix, iy = lax.axis_index("gx"), lax.axis_index("gy")
    after = {"gx": lax.rem(ix + 1, count_x)}
    before = {"gx": lax.rem(ix + count_x - 1, count_x)}
    above = {"gy": lax.rem(iy + 1, count_y)}
    below = {"gy": lax.rem(iy + count_y - 1, count_y)}

    loads = [
        pltpu.make_async_copy(rs_flat, raw, in_sem.at[0]),
        pltpu.make_async_copy(mat_flat, mat, in_sem.at[1]),
    ]
    for copy in loads:
        copy.start()

    barrier = pltpu.get_barrier_semaphore()
    for there in (after, before, above, below):
        pl.semaphore_signal(barrier, inc=1, device_id=there, device_id_type=MESH)
    pl.semaphore_wait(barrier, 4)

    span = depth // CHUNKS

    def bulk(chunk):
        zs = pl.ds(chunk * span, span)
        copies = []
        for side, there, first_row in ((0, after, rows - 2), (1, before, 0)):
            for k in range(2):
                slot = 2 * side + k
                copies.append(
                    pltpu.make_async_remote_copy(
                        src_ref=rs_hbm.at[:, zs, first_row + k, :],
                        dst_ref=halo_rs.at[slot, :, zs, :],
                        send_sem=x_send.at[chunk, slot, 0],
                        recv_sem=x_recv.at[chunk, slot, 0],
                        device_id=there,
                        device_id_type=MESH,
                    )
                )
                copies.append(
                    pltpu.make_async_remote_copy(
                        src_ref=mat_hbm.at[zs, first_row + k, :],
                        dst_ref=halo_mat.at[slot, zs, :],
                        send_sem=x_send.at[chunk, slot, 1],
                        recv_sem=x_recv.at[chunk, slot, 1],
                        device_id=there,
                        device_id_type=MESH,
                    )
                )
        return copies

    for chunk in range(CHUNKS):
        for copy in bulk(chunk):
            copy.start()

    zeros = jnp.zeros((TILE, LANES), jnp.float32)
    for name in PADDED:
        for row in range(ROWS + 1):
            bufs[name][row, 0:PAD, :] = zeros
            bufs[name][row, PAD + depth : 2 * PAD + depth, :] = zeros

    lane = lax.broadcasted_iota(jnp.int32, (TILE, LANES), 1)
    sub = lax.broadcasted_iota(jnp.int32, (TILE, LANES), 0)
    place = lane % GROUP
    row_of = lane // GROUP
    low_x = ix > 0
    high_x = ix < count_x - 1
    low_y = iy > 0
    high_y = iy < count_y - 1
    to_f32 = lambda flag: jnp.where(flag, 1.0, 0.0).astype(jnp.float32)
    inside_x = ((row_of >= 2) | low_x) & ((row_of < 10) | high_x)
    inside_y = ((place >= 2) | low_y) & ((place < 6) | high_y)
    band_mask = to_f32(inside_x & inside_y)
    mask_low, mask_high = to_f32(low_x), to_f32(high_x)

    def mask_of(row):
        if row == BAND:
            return band_mask
        if row < 2:
            return mask_low
        if row >= 10:
            return mask_high
        return None

    def masked(value, row):
        mask = mask_of(row)
        return value if mask is None else value * mask

    def sigma_of(kind):
        level = [cond[k] for k in range(16)]
        for bit in range(4):
            flag = (kind & (1 << bit)) != 0
            level = [
                jnp.where(flag, level[2 * k + 1], level[2 * k])
                for k in range(len(level) // 2)
            ]
        return level[0]

    for copy in loads:
        copy.wait()

    def prepare(j, carry):
        z0 = pl.multiple_of(j * TILE, TILE)
        packed = [zeros] * 4
        for x in range(rows):
            row = x + 2
            here = pl.ds(z0 * rows + x, TILE, stride=rows)
            sigma = sigma_of(mat[here, :])
            bufs["sg"][row, pl.ds(PAD + z0, TILE), :] = sigma
            chosen = (lane >= GROUP * row + 2) & (lane < GROUP * row + 6)
            for f in range(4):
                value = sigma if f == 3 else raw[f, here, :]
                packed[f] = jnp.where(chosen, roll(value, GROUP * row + 4), packed[f])
        for f in range(4):
            pack[f, pl.ds(z0, TILE), :] = packed[f]
        return carry

    lax.fori_loop(0, tiles, prepare, 0)

    def swap_y(side):
        return pltpu.make_async_remote_copy(
            src_ref=pack,
            dst_ref=pack_recv.at[side],
            send_sem=y_send.at[side],
            recv_sem=y_recv.at[side],
            device_id=(above, below)[side],
            device_id_type=MESH,
        )

    for side in range(2):
        swap_y(side).start()
    for side in range(2):
        swap_y(side).wait()

    half = depth // 2

    def assemble(j, carry):
        z0 = pl.multiple_of(j * TILE, TILE)
        zs = pl.ds(z0, TILE)
        for f in range(4):
            own = pack[f, zs, :]
            left = jnp.where(place < 4, pack_recv[0, f, zs, :], own)
            right = jnp.where(place < 4, own, pack_recv[1, f, zs, :])
            band[f, zs, :] = jnp.where(place < 4, roll(left, -2), roll(right, 2))
        return carry

    lax.fori_loop(0, tiles, assemble, 0)

    def cut(j, carry):
        z0 = pl.multiple_of(j * TILE, TILE)
        for side, start in ((0, 8 * GROUP), (1, 2 * GROUP)):
            value = zeros
            for h in range(2):
                for f in range(4):
                    at = 64 * h + 16 * f
                    source = band[f, pl.ds(h * half + z0, TILE), :]
                    value = jnp.where(
                        (lane >= at) & (lane < at + 16), roll(source, at - start), value
                    )
            corner[side, pl.ds(z0, TILE), :] = value
        return carry

    lax.fori_loop(0, tiles // 2, cut, 0)

    def swap_c(side):
        return pltpu.make_async_remote_copy(
            src_ref=corner.at[side],
            dst_ref=corner_recv.at[side],
            send_sem=c_send.at[side],
            recv_sem=c_recv.at[side],
            device_id=(after, before)[side],
            device_id_type=MESH,
        )

    for side in range(2):
        swap_c(side).start()
    for side in range(2):
        swap_c(side).wait()

    def paste(j, carry):
        z0 = pl.multiple_of(j * TILE, TILE)
        for h in range(2):
            zs = pl.ds(h * half + z0, TILE)
            for f in range(4):
                at = 64 * h + 16 * f
                value = band[f, zs, :]
                low = roll(corner_recv[0, pl.ds(z0, TILE), :], -at)
                high = roll(corner_recv[1, pl.ds(z0, TILE), :], 10 * GROUP - at)
                value = jnp.where(lane < 2 * GROUP, low, value)
                value = jnp.where(
                    (lane >= 10 * GROUP) & (lane < 12 * GROUP), high, value
                )
                band[f, zs, :] = value
        return carry

    lax.fori_loop(0, tiles // 2, paste, 0)

    class Tile:
        def __init__(self, z0):
            self.z0 = z0
            self.seen = {}
            self.bands = {}

        def load(self, name, row, dz=0):
            key = (name, row, dz)
            if key not in self.seen:
                self.seen[key] = bufs[name][row, pl.ds(PAD + self.z0 + dz, TILE), :]
            return self.seen[key]

        def store(self, name, row, value):
            bufs[name][row, pl.ds(PAD + self.z0, TILE), :] = value
            self.seen[(name, row, 0)] = value

        def up(self, value, row, edge):
            if row == BAND:
                return roll(value, -1)
            return jnp.where(
                lane == LANES - 1, roll(edge, LANES - 1 - (GROUP * row + 6)), roll(value, -1)
            )

        def down(self, value, row, edge):
            if row == BAND:
                return roll(value, 1)
            return jnp.where(lane == 0, roll(edge, -(GROUP * row + 1)), roll(value, 1))

    def next_x(get, row):
        return roll(get(BAND), -GROUP) if row == BAND else get(row + 1)

    def prior_x(get, row):
        return roll(get(BAND), GROUP) if row == BAND else get(row - 1)

    def each(low, high):
        return [BAND] + list(range(low, high + 1))

    four_x_band = 4.0 * roll(band_mask, GROUP)
    four_y_band = 4.0 * roll(band_mask, 1)
    four_y_main = jnp.where((lane == 0) & (iy == 0), 0.0, 4.0)

    def four_x(row):
        if row == BAND:
            return four_x_band
        mask = mask_of(row - 1)
        return 4.0 if mask is None else 4.0 * mask

    def pass_a(j, carry):
        z0 = pl.multiple_of(j * TILE, TILE)
        t = Tile(z0)
        zs = pl.ds(z0, TILE)
        for row in each(0, 11):
            if row == BAND:
                source = [band[f, zs, :] for f in range(3)]
                sigma = band[3, zs, :] * band_mask
            elif 2 <= row < 10:
                here = pl.ds(z0 * rows + row - 2, TILE, stride=rows)
                source = [raw[f, here, :] for f in range(3)]
                sigma = t.load("sg", row)
            else:
                slot = row if row < 2 else row - 8
                source = [halo_rs[slot, f, zs, :] for f in range(3)]
                sigma = masked(sigma_of(halo_mat[slot, zs, :]), row)
            scale = OMEGA_EDGE / (4.0 + sigma)
            left = masked(1.0 - sigma * scale, row)
            scale = masked(scale, row)
            for d, value in zip("xyz", source):
                t.store("f" + d, row, value * scale)
                t.store("t" + d, row, value * left)
            if not 2 <= row < 10:
                t.store("sg", row, sigma)
        sg = functools.partial(t.load, "sg")
        tx = functools.partial(t.load, "tx")
        for row in each(1, 11):
            sigma_y = t.down(sg(row), row, sg(BAND))
            t.store("sy", row, sigma_y)
            total = (
                (prior_x(tx, row) - tx(row))
                + (t.down(t.load("ty", row), row, t.load("ty", BAND)) - t.load("ty", row))
                + (t.load("tz", row, -1) - t.load("tz", row))
            )
            nodal = 3.0 * sg(row) + prior_x(sg, row) + sigma_y + t.load("sg", row, -1)
            mask = mask_of(row)
            if mask is not None:
                nodal = nodal + (1.0 - mask)
            weight = masked(OMEGA_NODE / nodal, row)
            t.store("p1", row, weight * total)
            t.store("rn", row, weight)
            t.store("nr", row, total)
        return carry

    def pass_b(j, carry):
        z0 = pl.multiple_of(j * TILE, TILE)
        t = Tile(z0)
        load = t.load
        get = lambda name: functools.partial(t.load, name)
        four_z = jnp.where((sub == 0) & (j == 0), 0.0, 4.0)
        for row in each(0, 10):
            fx, fy, fz = load("fx", row), load("fy", row), load("fz", row)
            face = fx - t.up(fx, row, load("fx", BAND)) + next_x(get("fy"), row) - fy
            t.store("gz", row, masked(face, row) if row < 2 or row == BAND else face)
            face = fz - next_x(get("fz"), row) + load("fx", row, 1) - fx
            t.store("gy", row, masked(face, row) if row < 2 or row == BAND else face)
            if row >= 1:
                face = fy - load("fy", row, 1) + t.up(fz, row, load("fz", BAND)) - fz
                t.store("gx", row, masked(face, row) if row < 2 or row == BAND else face)
        for row in each(0, 10):
            gz, gy = load("gz", row), load("gy", row)
            value = load("tx", row) - (
                gz - t.down(gz, row, load("gz", BAND)) - gy + load("gy", row, -1)
            )
            t.store("rx", row, masked(value, row) if row == BAND else value)
            if row >= 1:
                gx = load("gx", row)
                value = load("ty", row) - (
                    prior_x(get("gz"), row) - gz + gx - load("gx", row, -1)
                )
                t.store("ry", row, masked(value, row) if row >= 10 else value)
                value = load("tz", row) - (
                    t.down(gx, row, load("gx", BAND)) - gx + gy - prior_x(get("gy"), row)
                )
                t.store("rz", row, masked(value, row) if row >= 10 else value)
        psi_x, psi_y = {}, {}
        for row in each(1, 10):
            sigma = load("sg", row)
            base = 4.0 + sigma
            rx, ry, rz = load("rx", row), load("ry", row), load("rz", row)
            value = (rx + prior_x(get("rx"), row)) * (
                0.5 / (base + prior_x(get("sg"), row) + four_x(row))
            )
            psi_x[row] = masked(value, row) if row >= 10 else value
            value = (ry + t.down(ry, row, load("ry", BAND))) * (
                0.5
                / (base + load("sy", row) + (four_y_band if row == BAND else four_y_main))
            )
            psi_y[row] = masked(value, row) if row == BAND else value
            value = (rz + load("rz", row, -1)) * (
                0.5 / (base + load("sg", row, -1) + four_z)
            )
            t.store("sz", row, value)
            t.store("py", row, psi_y[row] + t.up(psi_y[row], row, psi_y[BAND]))
        for row in each(1, 9):
            t.store("px", row, psi_x[row] + next_x(lambda r: psi_x[r], row))
        flux = {}
        p1 = get("p1")
        for row in each(1, 10):
            flux[row] = load("sg", row) * (next_x(p1, row) - p1(row))
        flux_y = {}
        for row in each(2, 10):
            sigma = load("sg", row)
            t.store("fl", row, sigma * (load("p1", row, 1) - p1(row)))
            flux_y[row] = sigma * (t.up(p1(row), row, p1(BAND)) - p1(row))
            total = (
                (prior_x(lambda r: flux[r], row) - flux[row])
                + (t.down(flux_y[row], row, flux_y[BAND]) - flux_y[row])
                + (load("fl", row, -1) - load("fl", row))
            )
            value = p1(row) + load("rn", row) * (load("nr", row) - total)
            t.store("p2", row, masked(value, row) if row >= 10 else value)
        return carry

    def pass_c(j, carry):
        z0 = pl.multiple_of(j * TILE, TILE)
        t = Tile(z0)
        load = t.load
        get = lambda name: functools.partial(t.load, name)
        for row in each(1, 10):
            t.store("pz", row, load("sz", row) + load("sz", row, 1))
        for row in each(1, 9):
            px, py, pz = load("px", row), load("py", row), load("pz", row)
            face = px - t.up(px, row, load("px", BAND)) + next_x(get("py"), row) - py
            t.store("qz", row, masked(face, row) if row < 2 or row == BAND else face)
            face = pz - next_x(get("pz"), row) + load("px", row, 1) - px
            t.store("qy", row, masked(face, row) if row < 2 or row == BAND else face)
            if row >= 2:
                face = py - load("py", row, 1) + t.up(pz, row, load("pz", BAND)) - pz
                t.store("qx", row, masked(face, row) if row == BAND else face)
        p2 = get("p2")
        for row in range(2, 10):
            here = pl.ds(z0 * rows + row - 2, TILE, stride=rows)
            sigma = load("sg", row)
            mid = p2(row)
            step = (
                next_x(p2, row) - mid + load("px", row),
                t.up(mid, row, p2(BAND)) - mid + load("py", row),
                load("p2", row, 1) - mid + load("pz", row),
            )
            qx, qy, qz = load("qx", row), load("qy", row), load("qz", row)
            curl = (
                qz - t.down(qz, row, load("qz", BAND)) - qy + load("qy", row, -1),
                prior_x(get("qz"), row) - qz + qx - load("qx", row, -1),
                t.down(qx, row, load("qx", BAND)) - qx + qy - prior_x(get("qy"), row),
            )
            for f, d in enumerate("xyz"):
                corr_out[f, here, :] = load("f" + d, row) + step[f]
                res_out[f, here, :] = load("r" + d, row) - curl[f] - sigma * step[f]
        return carry

    width = tiles // CHUNKS

    def sweep(c, carry):
        @pl.when(c < CHUNKS)
        def _():
            for copy in bulk(c):
                copy.wait_recv()

        first = c * width
        lax.fori_loop(first, jnp.minimum(first + width, tiles), pass_a, 0)
        lax.fori_loop(
            jnp.maximum(first - 1, 0), jnp.minimum(first + width - 1, tiles), pass_b, 0
        )
        lax.fori_loop(
            jnp.maximum(first - 2, 0), jnp.minimum(first + width - 2, tiles), pass_c, 0
        )
        return carry

    lax.fori_loop(0, CHUNKS + 1, sweep, 0)

    for chunk in range(CHUNKS):
        for copy in bulk(chunk):
            copy.wait_send()


def solution(mesh):
    count_x, count_y = mesh.shape["gx"], mesh.shape["gy"]

    def local(right_side, material, conductivity):
        depth, rows, cols = material.shape
        flat = depth * rows
        f32 = jnp.float32
        out = jax.ShapeDtypeStruct((3, flat, cols), f32)
        dma = pltpu.SemaphoreType.DMA
        vmem = pl.BlockSpec(memory_space=pltpu.VMEM)
        anywhere = pl.BlockSpec(memory_space=pl.ANY)
        corrected, final = pl.pallas_call(
            functools.partial(kernel, (count_x, count_y, depth, rows, cols)),
            out_shape=(out, out),
            in_specs=[pl.BlockSpec(memory_space=pltpu.SMEM)] + [anywhere] * 4,
            out_specs=(vmem, vmem),
            scratch_shapes=[
                pltpu.VMEM((3, flat, cols), f32),
                pltpu.VMEM((flat, cols), jnp.int32),
                pltpu.VMEM((4, 3, depth, cols), f32),
                pltpu.VMEM((4, depth, cols), jnp.int32),
                pltpu.VMEM((4, depth, LANES), f32),
                pltpu.VMEM((2, 4, depth, LANES), f32),
                pltpu.VMEM((2, depth // 2, LANES), f32),
                pltpu.VMEM((2, depth // 2, LANES), f32),
                pltpu.VMEM((4, depth, LANES), f32),
            ]
            + [pltpu.VMEM((ROWS + 1, depth + 2 * PAD, LANES), f32)] * len(NAMES)
            + [
                dma((2,)),
                dma((CHUNKS, 4, 2)),
                dma((CHUNKS, 4, 2)),
                dma((2,)),
                dma((2,)),
                dma((2,)),
                dma((2,)),
            ],
            compiler_params=pltpu.CompilerParams(
                collective_id=0, has_side_effects=True, vmem_limit_bytes=40 << 20
            ),
        )(
            conductivity,
            right_side,
            right_side.reshape(3, flat, cols),
            material,
            material.reshape(flat, cols),
        )
        shape = (3, depth, rows, cols)
        return corrected.reshape(shape), final.reshape(shape)

    return jax.shard_map(
        local,
        mesh=mesh,
        in_specs=(P(None, None, "gx", "gy"), P(None, "gx", "gy"), P()),
        out_specs=(P(None, None, "gx", "gy"), P(None, None, "gx", "gy")),
        check_vma=False,
    )
```

time: 134 us -> 33.2 us (0.25)
  the two profiles are of different devices: /device:TPU:24 before, /device:TPU:16 now
where the time goes in v1:
time: 33.2 us; the launch traced here: 33 us
  Pallas kernels  27.9 us (84%)
  local copies, waits for them, and re-layouts  4.49 us (14%)
  between operations  0.65 us (2%)
    pallas_call x1, Pallas kernels, local(): pl.pallas_call(functools.partial(kernel, (count_x, count_y, depth, rows,...  27.9 us
    unnamed x8, local copies, waits for them, and re-layouts  4.49 us

profile of v1, /device:TPU:16, one launch (start us, length us, event | category | flops | bytes accessed | tf_op | source)
XLA Modules:
  0.0 33.0 jit_solution(2249927877816499190)
XLA Ops:
  0.6 0.0 copy-start.2
  0.6 0.6 %copy-done.2 = f32[16]{0:T(128)S(1)} copy-done((f32[16]{0:T(128)S(1)}, f32[16]{0:T(128)}, u32[]{:S(2)}) %copy-start.2) | copy-done | bytes 88
  1.3 0.0 copy-start
  1.3 1.1 %copy-done = f32[3,64,8,128]{3,2,1,0:T(8,128)S(1)} copy-done((f32[3,64,8,128]{3,2,1,0:T(8,128)S(1)}, f32[3,64,8,128]{3,2,1,0:T(8,128)}, u32[]{:S(2)}) %copy-start) | copy-done | bytes 786456
  2.4 0.0 copy-start.1
  2.4 0.9 %copy-done.1 = s32[64,8,128]{2,1,0:T(8,128)S(1)} copy-done((s32[64,8,128]{2,1,0:T(8,128)S(1)}, s32[64,8,128]{2,1,0:T(8,128)}, u32[]{:S(2)}) %copy-start.1) | copy-done | bytes 262168
  3.4 27.9 %shard_map.50 = (f32[3,512,128]{2,1,0:T(8,128)S(1)}, f32[3,512,128]{2,1,0:T(8,128)S(1)}) custom-call(f32[16]{0:T(128)S(1)} %copy-done.2, f32[3,64,8,128]{3,2,1,0:T(8,128)S(1)} %copy-done, f32[3,512,128]{2,1,0:T(8,128)S(1)} %bitcast.4, s32[64,8,128]{2,1,0:T(8,128)S(1)} %copy-done.1, s32[512,128]{1,0:T(8,128)S(1)} %bitcast.5), custom_call_target="tpu_custom_call" | custom-call | tf_op jit(solution)/shard_map/pallas_call | solution.py:489
  31.2 0.9 %copy.7 = f32[3,64,8,128]{3,2,1,0:T(8,128)} copy(f32[3,64,8,128]{3,2,1,0:T(8,128)S(1)} %bitcast.7) | data formatting | bytes 1572864
  32.1 0.9 %copy.8 = f32[3,64,8,128]{3,2,1,0:T(8,128)} copy(f32[3,64,8,128]{3,2,1,0:T(8,128)S(1)} %bitcast.6) | data formatting | bytes 1572864
Async XLA Ops:
  0.6 0.7 %copy-start.2 = (f32[16]{0:T(128)S(1)}, f32[16]{0:T(128)}, u32[]{:S(2)}) copy-start(f32[16]{0:T(128)} %cond.1) | copy-start | bytes 196
  1.3 1.1 %copy-start = (f32[3,64,8,128]{3,2,1,0:T(8,128)S(1)}, f32[3,64,8,128]{3,2,1,0:T(8,128)}, u32[]{:S(2)}) copy-start(f32[3,64,8,128]{3,2,1,0:T(8,128)} %rs_hbm.1) | copy-start | bytes 2359300
  2.4 0.9 %copy-start.1 = (s32[64,8,128]{2,1,0:T(8,128)S(1)}, s32[64,8,128]{2,1,0:T(8,128)}, u32[]{:S(2)}) copy-start(s32[64,8,128]{2,1,0:T(8,128)} %mat_hbm.1) | copy-start | bytes 786436

commit v2 on v1

--- a/solution.py
+++ b/solution.py
@@ -16,6 +16,7 @@
 BAND = 12
 GROUP = 8
 CHUNKS = 4
+EARLY = 2
 MESH = pl.DeviceIdType.MESH
 
 NAMES = (
@@ -34,24 +35,29 @@
     return value if shift == 0 else pltpu.roll(value, shift, 1)
 
 
+def turn(value, shift):
+    return pltpu.roll(value, lax.rem(shift + 2 * LANES, LANES), 1)
+
+
 def kernel(
     sizes,
-    cond,
+    cond_hbm,
     rs_hbm,
     rs_flat,
     mat_hbm,
     mat_flat,
     corr_out,
     res_out,
+    cond,
     raw,
     mat,
     halo_rs,
     halo_mat,
     pack,
-    pack_recv,
+    side_msg,
+    side_recv,
     corner,
     corner_recv,
-    band,
     *rest,
 ):
     bufs = dict(zip(NAMES, rest[: len(NAMES)]))
@@ -59,29 +65,36 @@
     count_x, count_y, depth, rows, cols = sizes
     tiles = depth // TILE
     ix, iy = lax.axis_index("gx"), lax.axis_index("gy")
-    after = {"gx": lax.rem(ix + 1, count_x)}
-    before = {"gx": lax.rem(ix + count_x - 1, count_x)}
-    above = {"gy": lax.rem(iy + 1, count_y)}
-    below = {"gy": lax.rem(iy + count_y - 1, count_y)}
+    east, west = lax.rem(ix + 1, count_x), lax.rem(ix + count_x - 1, count_x)
+    north, south = lax.rem(iy + 1, count_y), lax.rem(iy + count_y - 1, count_y)
+    x_sides = ({"gx": east, "gy": iy}, {"gx": west, "gy": iy})
+    y_sides = ({"gx": ix, "gy": north}, {"gx": ix, "gy": south})
+    diagonals = (
+        {"gx": east, "gy": north},
+        {"gx": east, "gy": south},
+        {"gx": west, "gy": north},
+        {"gx": west, "gy": south},
+    )
 
     loads = [
+        pltpu.make_async_copy(cond_hbm, cond, in_sem.at[2]),
+        pltpu.make_async_copy(mat_flat, mat, in_sem.at[1]),
         pltpu.make_async_copy(rs_flat, raw, in_sem.at[0]),
-        pltpu.make_async_copy(mat_flat, mat, in_sem.at[1]),
     ]
     for copy in loads:
         copy.start()
 
     barrier = pltpu.get_barrier_semaphore()
-    for there in (after, before, above, below):
+    for there in x_sides + y_sides + diagonals:
         pl.semaphore_signal(barrier, inc=1, device_id=there, device_id_type=MESH)
-    pl.semaphore_wait(barrier, 4)
+    pl.semaphore_wait(barrier, 8)
 
     span = depth // CHUNKS
 
     def bulk(chunk):
         zs = pl.ds(chunk * span, span)
         copies = []
-        for side, there, first_row in ((0, after, rows - 2), (1, before, 0)):
+        for side, first_row in ((0, rows - 2), (1, 0)):
             for k in range(2):
                 slot = 2 * side + k
                 copies.append(
@@ -90,7 +103,7 @@
                         dst_ref=halo_rs.at[slot, :, zs, :],
                         send_sem=x_send.at[chunk, slot, 0],
                         recv_sem=x_recv.at[chunk, slot, 0],
-                        device_id=there,
+                        device_id=x_sides[side],
                         device_id_type=MESH,
                     )
                 )
@@ -100,22 +113,17 @@
                         dst_ref=halo_mat.at[slot, zs, :],
                         send_sem=x_send.at[chunk, slot, 1],
                         recv_sem=x_recv.at[chunk, slot, 1],
-                        device_id=there,
+                        device_id=x_sides[side],
                         device_id_type=MESH,
                     )
                 )
         return copies
 
-    for chunk in range(CHUNKS):
+    for chunk in range(EARLY):
         for copy in bulk(chunk):
             copy.start()
 
     zeros = jnp.zeros((TILE, LANES), jnp.float32)
-    for name in PADDED:
-        for row in range(ROWS + 1):
-            bufs[name][row, 0:PAD, :] = zeros
-            bufs[name][row, PAD + depth : 2 * PAD + depth, :] = zeros
-
     lane = lax.broadcasted_iota(jnp.int32, (TILE, LANES), 1)
     sub = lax.broadcasted_iota(jnp.int32, (TILE, LANES), 0)
     place = lane % GROUP
@@ -143,18 +151,21 @@
         mask = mask_of(row)
         return value if mask is None else value * mask
 
-    def sigma_of(kind):
-        level = [cond[k] for k in range(16)]
-        for bit in range(4):
-            flag = (kind & (1 << bit)) != 0
-            level = [
-                jnp.where(flag, level[2 * k + 1], level[2 * k])
-                for k in range(len(level) // 2)
-            ]
-        return level[0]
-
     for copy in loads:
         copy.wait()
+
+    table = zeros
+    for k in range(16):
+        table = jnp.where(lane == k, cond[k], table)
+
+    def sigma_of(kind):
+        return jnp.take_along_axis(table, kind, axis=1, mode="promise_in_bounds")
+
+    def ends(values, row, packed):
+        chosen = (lane >= GROUP * row + 2) & (lane < GROUP * row + 6)
+        return [
+            jnp.where(chosen, roll(v, GROUP * row + 4), p) for v, p in zip(values, packed)
+        ]
 
     def prepare(j, carry):
         z0 = pl.multiple_of(j * TILE, TILE)
@@ -164,93 +175,64 @@
             here = pl.ds(z0 * rows + x, TILE, stride=rows)
             sigma = sigma_of(mat[here, :])
             bufs["sg"][row, pl.ds(PAD + z0, TILE), :] = sigma
-            chosen = (lane >= GROUP * row + 2) & (lane < GROUP * row + 6)
-            for f in range(4):
-                value = sigma if f == 3 else raw[f, here, :]
-                packed[f] = jnp.where(chosen, roll(value, GROUP * row + 4), packed[f])
+            packed = ends([raw[f, here, :] for f in range(3)] + [sigma], row, packed)
+        up, down = zeros, zeros
         for f in range(4):
             pack[f, pl.ds(z0, TILE), :] = packed[f]
+            mine = place // 2 == f
+            up = jnp.where(mine, roll(packed[f], 2 * f - 2), up)
+            down = jnp.where(mine, roll(packed[f], 2 * f - 4), down)
+        side_msg[pl.ds(z0, TILE), :] = jnp.where(
+            (lane >= 16) & (lane < 80), up, roll(down, 64)
+        )
         return carry
 
     lax.fori_loop(0, tiles, prepare, 0)
 
-    def swap_y(side):
-        return pltpu.make_async_remote_copy(
-            src_ref=pack,
-            dst_ref=pack_recv.at[side],
-            send_sem=y_send.at[side],
-            recv_sem=y_recv.at[side],
-            device_id=(above, below)[side],
-            device_id_type=MESH,
-        )
-
-    for side in range(2):
-        swap_y(side).start()
-    for side in range(2):
-        swap_y(side).wait()
-
-    half = depth // 2
-
-    def assemble(j, carry):
-        z0 = pl.multiple_of(j * TILE, TILE)
-        zs = pl.ds(z0, TILE)
-        for f in range(4):
-            own = pack[f, zs, :]
-            left = jnp.where(place < 4, pack_recv[0, f, zs, :], own)
-            right = jnp.where(place < 4, own, pack_recv[1, f, zs, :])
-            band[f, zs, :] = jnp.where(place < 4, roll(left, -2), roll(right, 2))
-        return carry
-
-    lax.fori_loop(0, tiles, assemble, 0)
-
-    def cut(j, carry):
-        z0 = pl.multiple_of(j * TILE, TILE)
-        for side, start in ((0, 8 * GROUP), (1, 2 * GROUP)):
-            value = zeros
-            for h in range(2):
-                for f in range(4):
-                    at = 64 * h + 16 * f
-                    source = band[f, pl.ds(h * half + z0, TILE), :]
-                    value = jnp.where(
-                        (lane >= at) & (lane < at + 16), roll(source, at - start), value
-                    )
-            corner[side, pl.ds(z0, TILE), :] = value
-        return carry
-
-    lax.fori_loop(0, tiles // 2, cut, 0)
-
-    def swap_c(side):
-        return pltpu.make_async_remote_copy(
-            src_ref=corner.at[side],
-            dst_ref=corner_recv.at[side],
-            send_sem=c_send.at[side],
-            recv_sem=c_recv.at[side],
-            device_id=(after, before)[side],
-            device_id_type=MESH,
-        )
-
-    for side in range(2):
-        swap_c(side).start()
-    for side in range(2):
-        swap_c(side).wait()
-
-    def paste(j, carry):
-        z0 = pl.multiple_of(j * TILE, TILE)
-        for h in range(2):
-            zs = pl.ds(h * half + z0, TILE)
-            for f in range(4):
-                at = 64 * h + 16 * f
-                value = band[f, zs, :]
-                low = roll(corner_recv[0, pl.ds(z0, TILE), :], -at)
-                high = roll(corner_recv[1, pl.ds(z0, TILE), :], 10 * GROUP - at)
-                value = jnp.where(lane < 2 * GROUP, low, value)
-                value = jnp.where(
-                    (lane >= 10 * GROUP) & (lane < 12 * GROUP), high, value
-                )
-                band[f, zs, :] = value
-        return carry
-
-    lax.fori_loop(0, tiles // 2, paste, 0)
+    for q, start in enumerate((64, 0, 16, 80)):
+        value = zeros
+        for k in range(tiles):
+            source = side_msg[TILE * k : TILE * (k + 1), :]
+            value = jnp.where(lane // 16 == k, roll(source, 16 * k - start), value)
+        corner[q] = value
+
+    def small():
+        copies = [
+            pltpu.make_async_remote_copy(
+                src_ref=corner.at[q],
+                dst_ref=corner_recv.at[q],
+                send_sem=c_send.at[q],
+                recv_sem=c_recv.at[q],
+                device_id=diagonals[q],
+                device_id_type=MESH,
+            )
+            for q in range(4)
+        ]
+        return copies + [
+            pltpu.make_async_remote_copy(
+                src_ref=side_msg,
+                dst_ref=side_recv.at[side],
+                send_sem=y_send.at[side],
+                recv_sem=y_recv.at[side],
+                device_id=y_sides[side],
+                device_id_type=MESH,
+            )
+            for side in range(2)
+        ]
+
+    for copy in small():
+        copy.start()
+    for chunk in range(EARLY, CHUNKS):
+        for copy in bulk(chunk):
+            copy.start()
+
+    for name in PADDED:
+        for row in range(ROWS + 1):
+            bufs[name][row, 0:PAD, :] = zeros
+            bufs[name][row, PAD + depth : 2 * PAD + depth, :] = zeros
+
+    for copy in small():
+        copy.wait_recv()
 
     class Tile:
         def __init__(self, z0):
@@ -303,22 +285,38 @@
         z0 = pl.multiple_of(j * TILE, TILE)
         t = Tile(z0)
         zs = pl.ds(z0, TILE)
-        for row in each(0, 11):
-            if row == BAND:
-                source = [band[f, zs, :] for f in range(3)]
-                sigma = band[3, zs, :] * band_mask
-            elif 2 <= row < 10:
+        sources = {}
+        packed = [pack[f, zs, :] for f in range(4)]
+        for row in range(ROWS):
+            if 2 <= row < 10:
                 here = pl.ds(z0 * rows + row - 2, TILE, stride=rows)
-                source = [raw[f, here, :] for f in range(3)]
-                sigma = t.load("sg", row)
+                sources[row] = [raw[f, here, :] for f in range(3)] + [t.load("sg", row)]
             else:
                 slot = row if row < 2 else row - 8
-                source = [halo_rs[slot, f, zs, :] for f in range(3)]
-                sigma = masked(sigma_of(halo_mat[slot, zs, :]), row)
+                sources[row] = [halo_rs[slot, f, zs, :] for f in range(3)] + [
+                    sigma_of(halo_mat[slot, zs, :])
+                ]
+                packed = ends(sources[row], row, packed)
+        low = jnp.where(lane < 80, side_recv[0, zs, :], turn(corner_recv[2], 80 - 16 * j))
+        low = jnp.where(lane < 16, turn(corner_recv[0], -16 * j), low)
+        high = jnp.where(
+            lane < 80, roll(side_recv[1, zs, :], 64), turn(corner_recv[3], 80 - 16 * j)
+        )
+        high = jnp.where(lane < 16, turn(corner_recv[1], -16 * j), high)
+        sources[BAND] = [
+            jnp.where(
+                place < 4,
+                jnp.where(place < 2, roll(low, -2 * f), roll(packed[f], -2)),
+                jnp.where(place < 6, roll(packed[f], 2), roll(high, 6 - 2 * f)),
+            )
+            for f in range(4)
+        ]
+        for row in each(0, 11):
+            sigma = masked(sources[row][3], row)
             scale = OMEGA_EDGE / (4.0 + sigma)
             left = masked(1.0 - sigma * scale, row)
             scale = masked(scale, row)
-            for d, value in zip("xyz", source):
+            for d, value in zip("xyz", sources[row]):
                 t.store("f" + d, row, value * scale)
                 t.store("t" + d, row, value * left)
             if not 2 <= row < 10:
@@ -470,9 +468,22 @@
 
     lax.fori_loop(0, CHUNKS + 1, sweep, 0)
 
+    for copy in small():
+        copy.wait_send()
     for chunk in range(CHUNKS):
         for copy in bulk(chunk):
             copy.wait_send()
+
+
+def leave(corr, res, corr_out, res_out, sem):
+    copies = [
+        pltpu.make_async_copy(source, target, sem.at[k])
+        for k, (source, target) in enumerate(((corr, corr_out), (res, res_out)))
+    ]
+    for copy in copies:
+        copy.start()
+    for copy in copies:
+        copy.wait()
 
 
 def solution(mesh):
@@ -485,43 +496,57 @@
         out = jax.ShapeDtypeStruct((3, flat, cols), f32)
         dma = pltpu.SemaphoreType.DMA
         vmem = pl.BlockSpec(memory_space=pltpu.VMEM)
-        anywhere = pl.BlockSpec(memory_space=pl.ANY)
+        hbm = pl.BlockSpec(memory_space=pltpu.HBM)
         corrected, final = pl.pallas_call(
             functools.partial(kernel, (count_x, count_y, depth, rows, cols)),
             out_shape=(out, out),
-            in_specs=[pl.BlockSpec(memory_space=pltpu.SMEM)] + [anywhere] * 4,
+            in_specs=[hbm] * 5,
             out_specs=(vmem, vmem),
             scratch_shapes=[
+                pltpu.SMEM((16,), f32),
                 pltpu.VMEM((3, flat, cols), f32),
                 pltpu.VMEM((flat, cols), jnp.int32),
                 pltpu.VMEM((4, 3, depth, cols), f32),
                 pltpu.VMEM((4, depth, cols), jnp.int32),
                 pltpu.VMEM((4, depth, LANES), f32),
-                pltpu.VMEM((2, 4, depth, LANES), f32),
-                pltpu.VMEM((2, depth // 2, LANES), f32),
-                pltpu.VMEM((2, depth // 2, LANES), f32),
-                pltpu.VMEM((4, depth, LANES), f32),
+                pltpu.VMEM((depth, LANES), f32),
+                pltpu.VMEM((2, depth, LANES), f32),
+                pltpu.VMEM((4, TILE, LANES), f32),
+                pltpu.VMEM((4, TILE, LANES), f32),
             ]
             + [pltpu.VMEM((ROWS + 1, depth + 2 * PAD, LANES), f32)] * len(NAMES)
             + [
-                dma((2,)),
+                dma((3,)),
                 dma((CHUNKS, 4, 2)),
                 dma((CHUNKS, 4, 2)),
                 dma((2,)),
                 dma((2,)),
-                dma((2,)),
-                dma((2,)),
+                dma((4,)),
+                dma((4,)),
             ],
             compiler_params=pltpu.CompilerParams(
                 collective_id=0, has_side_effects=True, vmem_limit_bytes=40 << 20
             ),
         )(
-            conductivity,
-            right_side,
-            right_side.reshape(3, flat, cols),
-            material,
-            material.reshape(flat, cols),
+            *(
+                pltpu.with_memory_space_constraint(value, pltpu.HBM)
+                for value in (
+                    conductivity,
+                    right_side,
+                    right_side.reshape(3, flat, cols),
+                    material,
+                    material.reshape(flat, cols),
+                )
+            )
         )
+        corrected, final = pl.pallas_call(
+            leave,
+            out_shape=(out, out),
+            in_specs=[vmem, vmem],
+            out_specs=(hbm, hbm),
+            scratch_shapes=[dma((2,))],
+            compiler_params=pltpu.CompilerParams(vmem_limit_bytes=1 << 20),
+        )(corrected, final)
         shape = (3, depth, rows, cols)
         return corrected.reshape(shape), final.reshape(shape)
 

time: 33.2 us -> 27.7 us (0.83)
  the two profiles are of different devices: /device:TPU:16 before, /device:TPU:1 now
where the time goes in v2:
time: 27.7 us; the launch traced here: 27.6 us
  Pallas kernels  26.9 us (97%)
  between operations  0.64 us (2%)
    pallas_call x1, Pallas kernels, local(): pl.pallas_call(functools.partial(kernel, (count_x, count_y, depth, rows,...  25.8 us
    pallas_call x1, Pallas kernels, local(): pl.pallas_call(leave, out_shape=(out, out), in_specs=[vmem, vmem], out_sp...  1.16 us

profile of v2, /device:TPU:1, one launch (start us, length us, event | category | flops | bytes accessed | tf_op | source)
XLA Modules:
  0.0 27.6 jit_solution(16764954805125427015)
XLA Ops:
  0.6 25.8 %shard_map.50 = (f32[3,512,128]{2,1,0:T(8,128)S(1)}, f32[3,512,128]{2,1,0:T(8,128)S(1)}) custom-call(f32[16]{0:T(128)} %cond_hbm.1, f32[3,64,8,128]{3,2,1,0:T(8,128)} %rs_hbm.1, f32[3,512,128]{2,1,0:T(8,128)} %bitcast.4, s32[64,8,128]{2,1,0:T(8,128)} %mat_hbm.1, s32[512,128]{1,0:T(8,128)} %bitcast.5), custom_call_target="tpu_custom_call" | custom-call | tf_op jit(solution)/shard_map/pallas_call | solution.py:500
  26.4 1.2 %shard_map.51 = (f32[3,512,128]{2,1,0:T(8,128)}, f32[3,512,128]{2,1,0:T(8,128)}) custom-call(f32[3,512,128]{2,1,0:T(8,128)S(1)} %get-tuple-element.6.corr, f32[3,512,128]{2,1,0:T(8,128)S(1)} %get-tuple-element.7.res), custom_call_target="tpu_custom_call" | custom-call | tf_op jit(solution)/shard_map/pallas_call | solution.py:542

commit v3 on v2

v3 whole, which is shorter than its diff:
```python
import functools

import jax
import jax.numpy as jnp
from jax import lax
from jax.experimental import pallas as pl
from jax.experimental.pallas import tpu as pltpu
from jax.sharding import PartitionSpec as P

OMEGA_EDGE = 0.6
OMEGA_NODE = 0.7
LANES = 128
TILE = 8
PAD = 8
ROWS = 12
BAND = 12
GROUP = 8
EARLY = 3
MESH = pl.DeviceIdType.MESH

NAMES = (
    "fx", "fy", "fz", "tx", "ty", "tz", "sg", "sy", "p1", "nr",
    "rn", "gz", "gx", "rx", "ry", "rz", "sz", "px", "py", "fl",
    "p2", "pz", "qz", "qx", "qy", "gy",
)
READ_BELOW = ("tz", "sg", "gy", "gx", "rz", "fl", "qy", "qx")
READ_ABOVE = ("fx", "fy", "p1", "p2", "sz", "px", "py")


def roll(value, shift):
    shift = shift % LANES
    return value if shift == 0 else pltpu.roll(value, shift, 1)


def turn(value, shift):
    return pltpu.roll(value, lax.rem(shift + 2 * LANES, LANES), 1)


def kernel(
    sizes,
    cond_hbm,
    rs_hbm,
    mat_hbm,
    corr_out,
    res_out,
    cond,
    raw,
    mat,
    halo_rs,
    halo_mat,
    pack,
    side_msg,
    side_recv,
    corner,
    corner_recv,
    *rest,
):
    bufs = dict(zip(NAMES, rest[: len(NAMES)]))
    in_sem, x_send, x_recv, y_send, y_recv, c_send, c_recv = rest[len(NAMES) :]
    count_x, count_y, depth, rows, cols = sizes
    tiles = depth // TILE
    ix, iy = lax.axis_index("gx"), lax.axis_index("gy")
    low_x, high_x = ix > 0, ix < count_x - 1
    low_y, high_y = iy > 0, iy < count_y - 1
    x_sides = ({"gx": ix + 1, "gy": iy}, {"gx": ix - 1, "gy": iy})
    x_there = (high_x, low_x)
    y_sides = ({"gx": ix, "gy": iy + 1}, {"gx": ix, "gy": iy - 1})
    y_there = (high_y, low_y)
    corners = (
        {"gx": ix + 1, "gy": iy + 1},
        {"gx": ix + 1, "gy": iy - 1},
        {"gx": ix - 1, "gy": iy + 1},
        {"gx": ix - 1, "gy": iy - 1},
    )
    c_there = (high_x & high_y, high_x & low_y, low_x & high_y, low_x & low_y)

    pltpu.make_async_copy(cond_hbm, cond, in_sem.at[2]).start()
    for x in range(rows):
        pltpu.make_async_copy(mat_hbm.at[:, x, :], mat.at[x], in_sem.at[1]).start()
        pltpu.make_async_copy(rs_hbm.at[:, :, x, :], raw.at[x], in_sem.at[0]).start()

    barrier = pltpu.get_barrier_semaphore()
    expected = 0
    for there, present in zip(
        x_sides + y_sides + corners, x_there + y_there + c_there
    ):
        expected = expected + jnp.where(present, 1, 0)

        @pl.when(present)
        def _():
            pl.semaphore_signal(barrier, inc=1, device_id=there, device_id_type=MESH)

    zeros = jnp.zeros((TILE, LANES), jnp.float32)

    for side in range(2):

        @pl.when(~x_there[1 - side])
        def _():
            halo_rs[2 * side : 2 * side + 2] = jnp.zeros((2, 3, depth, LANES), jnp.float32)
            halo_mat[2 * side : 2 * side + 2] = jnp.zeros((2, depth, LANES), jnp.int32)

        @pl.when(~y_there[1 - side])
        def _():
            side_recv[side] = jnp.zeros((depth, LANES), jnp.float32)

    for q in range(4):

        @pl.when(~c_there[3 - q])
        def _():
            corner_recv[q] = zeros

    def bulk(side, z0):
        zs = pl.ds(z0, TILE)
        first_row = (rows - 2, 0)[side]
        j = z0 // TILE
        copies = []
        for k in range(2):
            slot = 2 * side + k
            for source, target, sem in (
                (rs_hbm.at[:, zs, first_row + k, :], halo_rs.at[slot, :, zs, :], 0),
                (mat_hbm.at[zs, first_row + k, :], halo_mat.at[slot, zs, :], 1),
            ):
                copies.append(
                    pltpu.make_async_remote_copy(
                        src_ref=source,
                        dst_ref=target,
                        send_sem=x_send.at[side, sem],
                        recv_sem=x_recv.at[j, side, sem],
                        device_id=x_sides[side],
                        device_id_type=MESH,
                    )
                )
        return copies

    def send_bulk(start, stop):
        for side in range(2):

            @pl.when(x_there[side])
            def _():
                for j in range(start, stop):
                    for copy in bulk(side, j * TILE):
                        copy.start()

    def wait_bytes(ref, sem):
        pltpu.make_async_copy(ref, ref, sem).wait()

    def wait_bulk(j):
        zs = pl.ds(j * TILE, TILE)
        for side in range(2):

            @pl.when(x_there[1 - side])
            def _():
                pair = pl.ds(2 * side, 2)
                wait_bytes(halo_rs.at[pair, :, zs, :], x_recv.at[j, side, 0])
                wait_bytes(halo_mat.at[pair, zs, :], x_recv.at[j, side, 1])

    lane = lax.broadcasted_iota(jnp.int32, (TILE, LANES), 1)
    sub = lax.broadcasted_iota(jnp.int32, (TILE, LANES), 0)
    place = lane % GROUP
    row_of = lane // GROUP
    to_f32 = lambda flag: jnp.where(flag, 1.0, 0.0).astype(jnp.float32)
    inside_x = ((row_of >= 2) | low_x) & ((row_of < 10) | high_x)
    inside_y = ((place >= 2) | low_y) & ((place < 6) | high_y)
    band_mask = to_f32(inside_x & inside_y)
    mask_low, mask_high = to_f32(low_x), to_f32(high_x)

    def mask_of(row):
        if row == BAND:
            return band_mask
        if row < 2:
            return mask_low
        if row >= 10:
            return mask_high
        return None

    def masked(value, row):
        mask = mask_of(row)
        return value if mask is None else value * mask

    def class_table():
        return [cond[k] for k in range(16)]

    def look_up(level, kind):
        for bit in range(4):
            flag = (kind & (1 << bit)) != 0
            level = [
                jnp.where(flag, level[2 * k + 1], level[2 * k])
                for k in range(len(level) // 2)
            ]
        return level[0]

    def ends(values, row, packed):
        chosen = (lane >= GROUP * row + 2) & (lane < GROUP * row + 6)
        return [
            jnp.where(chosen, roll(v, GROUP * row + 4), p) for v, p in zip(values, packed)
        ]

    def start_row(row, values, there, keep_sigma=True):
        sigma = masked(values[3], row)
        scale = OMEGA_EDGE / (4.0 + sigma)
        left = masked(1.0 - sigma * scale, row)
        scale = masked(scale, row)
        for d, value in zip("xyz", values):
            bufs["f" + d][row, there, :] = value * scale
            bufs["t" + d][row, there, :] = value * left
        bufs["sg"][row, there, :] = sigma

    def prepare_all():
        pltpu.make_async_copy(cond_hbm, cond, in_sem.at[2]).wait()
        wait_bytes(mat, in_sem.at[1])
        wait_bytes(raw, in_sem.at[0])
        table = class_table()

        def prepare(j, carry):
            z0 = pl.multiple_of(j * TILE, TILE)
            zs = pl.ds(z0, TILE)
            packed = [zeros] * 4
            for x in range(rows):
                values = [raw[x, f, zs, :] for f in range(3)]
                values.append(look_up(table, mat[x, zs, :]))
                start_row(x + 2, values, pl.ds(PAD + z0, TILE))
                packed = ends(values, x + 2, packed)
            up, down = zeros, zeros
            for f in range(4):
                pack[f, zs, :] = packed[f]
                mine = place // 2 == f
                up = jnp.where(mine, roll(packed[f], 2 * f - 2), up)
                down = jnp.where(mine, roll(packed[f], 2 * f - 4), down)
            side_msg[zs, :] = jnp.where((lane >= 16) & (lane < 80), up, roll(down, 64))
            return carry

        lax.fori_loop(0, tiles, prepare, 0)
        for q, start in enumerate((64, 0, 16, 80)):
            value = zeros
            for k in range(tiles):
                source = side_msg[TILE * k : TILE * (k + 1), :]
                value = jnp.where(lane // 16 == k, roll(source, 16 * k - start), value)
            corner[q] = value
        for row in range(ROWS + 1):
            for name in READ_BELOW:
                bufs[name][row, 0:PAD, :] = zeros
            for name in READ_ABOVE:
                bufs[name][row, PAD + depth : 2 * PAD + depth, :] = zeros

    def corner_copy(q):
        return pltpu.make_async_remote_copy(
            src_ref=corner.at[q],
            dst_ref=corner_recv.at[q],
            send_sem=c_send.at[q],
            recv_sem=c_recv.at[q],
            device_id=corners[q],
            device_id_type=MESH,
        )

    def side_copy(side):
        return pltpu.make_async_remote_copy(
            src_ref=side_msg,
            dst_ref=side_recv.at[side],
            send_sem=y_send.at[side],
            recv_sem=y_recv.at[side],
            device_id=y_sides[side],
            device_id_type=MESH,
        )

    period = max(count_x // 2, 2)
    early = lax.rem(ix, period) < period // 2
    pl.when(early)(prepare_all)
    pl.semaphore_wait(barrier, expected)
    send_bulk(0, EARLY)
    pl.when(~early)(prepare_all)
    for q in range(4):

        @pl.when(c_there[q])
        def _():
            corner_copy(q).start()

    for side in range(2):

        @pl.when(y_there[side])
        def _():
            side_copy(side).start()

    send_bulk(EARLY, tiles)
    table = class_table()
    for q in range(4):

        @pl.when(c_there[3 - q])
        def _():
            corner_copy(q).wait_recv()

    for side in range(2):

        @pl.when(y_there[1 - side])
        def _():
            side_copy(side).wait_recv()

    class Tile:
        def __init__(self, z0):
            self.z0 = z0
            self.seen = {}

        def load(self, name, row, dz=0):
            key = (name, row, dz)
            if key not in self.seen:
                self.seen[key] = bufs[name][row, pl.ds(PAD + self.z0 + dz, TILE), :]
            return self.seen[key]

        def store(self, name, row, value):
            bufs[name][row, pl.ds(PAD + self.z0, TILE), :] = value
            self.seen[(name, row, 0)] = value

        def get(self, name):
            return functools.partial(self.load, name)

    def pair(first, second):
        return jnp.where(place == 3, first, second)

    def border(both, row):
        return None if row == BAND else roll(both, LANES - 1 - (GROUP * row + 3))

    def up(value, edge):
        value = roll(value, -1)
        return value if edge is None else jnp.where(lane == LANES - 1, edge, value)

    def down(value, edge):
        value = roll(value, 1)
        return value if edge is None else jnp.where(lane == 0, edge, value)

    def down_early(value, edge):
        if edge is not None:
            value = jnp.where(lane == LANES - 1, edge, value)
        return roll(value, 1)

    def next_x(get, row):
        return roll(get(BAND), -GROUP) if row == BAND else get(row + 1)

    def prior_x(get, row):
        return roll(get(BAND), GROUP) if row == BAND else get(row - 1)

    four_x_band = 4.0 + 4.0 * roll(band_mask, GROUP)
    four_y_band = 4.0 + 4.0 * roll(band_mask, 1)
    four_y_main = jnp.where((lane == 0) & ~low_y, 4.0, 8.0)

    def four_x(row):
        if row == BAND:
            return four_x_band
        mask = mask_of(row - 1)
        return 8.0 if mask is None else 4.0 + 4.0 * mask

    def pass_a(j):
        z0 = pl.multiple_of(j * TILE, TILE)
        t = Tile(z0)
        zs = pl.ds(z0, TILE)
        there = pl.ds(PAD + z0, TILE)
        packed = [pack[f, zs, :] for f in range(4)]
        for row in (0, 1, 10, 11):
            slot = row if row < 2 else row - 8
            values = [halo_rs[slot, f, zs, :] for f in range(3)]
            values.append(look_up(table, halo_mat[slot, zs, :]))
            start_row(row, values, there)
            packed = ends(values, row, packed)
        low = jnp.where(lane < 80, side_recv[0, zs, :], turn(corner_recv[2], 80 - 16 * j))
        low = jnp.where(lane < 16, turn(corner_recv[0], -16 * j), low)
        high = jnp.where(
            lane < 80, roll(side_recv[1, zs, :], 64), turn(corner_recv[3], 80 - 16 * j)
        )
        high = jnp.where(lane < 16, turn(corner_recv[1], -16 * j), high)
        values = [
            jnp.where(
                place < 4,
                jnp.where(place < 2, roll(low, -2 * f), roll(packed[f], -2)),
                jnp.where(place < 6, roll(packed[f], 2), roll(high, 6 - 2 * f)),
            )
            for f in range(4)
        ]
        start_row(BAND, values, there)
        sg, tx = t.get("sg"), t.get("tx")
        both = pair(roll(t.load("ty", BAND), 2), roll(sg(BAND), 3))
        for row in [BAND] + list(range(1, 12)):
            edge = border(both, row)
            sigma_y = down(sg(row), edge)
            t.store("sy", row, sigma_y)
            ty = t.load("ty", row)
            total = (
                (prior_x(tx, row) - tx(row))
                + (down_early(ty, edge) - ty)
                + (t.load("tz", row, -1) - t.load("tz", row))
            )
            nodal = 3.0 * sg(row) + prior_x(sg, row) + sigma_y + t.load("sg", row, -1)
            mask = mask_of(row)
            if mask is not None:
                nodal = nodal + (1.0 - mask)
            weight = masked(OMEGA_NODE / nodal, row)
            t.store("p1", row, weight * total)
            t.store("rn", row, weight)
            t.store("nr", row, total)

    def pass_b(j):
        z0 = pl.multiple_of(j * TILE, TILE)
        t = Tile(z0)
        load = t.load
        four_z = jnp.where((sub == 0) & (j == 0), 4.0, 8.0)
        edges = {}
        psi_x, flux_x = {}, {}

        def faces(row):
            fx, fy, fz = load("fx", row), load("fy", row), load("fz", row)
            outer = row < 2 or row == BAND
            edge = edges.get(("fx", row))
            face = fx - up(fx, edge) + next_x(t.get("fy"), row) - fy
            t.store("gz", row, masked(face, row) if outer else face)
            face = fz - next_x(t.get("fz"), row) + load("fx", row, 1) - fx
            t.store("gy", row, masked(face, row) if outer else face)
            if row >= 1:
                edge = edges.get(("fz", row))
                face = fy - load("fy", row, 1) + up(fz, edge) - fz
                t.store("gx", row, masked(face, row) if outer else face)

        def residual(row):
            gz, gy = load("gz", row), load("gy", row)
            value = load("tx", row) - (
                gz - down(gz, edges.get(("fx", row))) - gy + load("gy", row, -1)
            )
            t.store("rx", row, masked(value, row) if row == BAND else value)
            if row >= 1:
                gx = load("gx", row)
                value = load("ty", row) - (
                    prior_x(t.get("gz"), row) - gz + gx - load("gx", row, -1)
                )
                t.store("ry", row, masked(value, row) if row >= 10 else value)
                value = load("tz", row) - (
                    down(gx, edges.get(("fz", row))) - gx + gy - prior_x(t.get("gy"), row)
                )
                t.store("rz", row, masked(value, row) if row >= 10 else value)

        def vector(row):
            sigma = load("sg", row)
            rx, ry, rz = load("rx", row), load("ry", row), load("rz", row)
            edge = edges.get(("sy", row))
            value = (rx + prior_x(t.get("rx"), row)) * (
                0.5 / (sigma + prior_x(t.get("sg"), row) + four_x(row))
            )
            psi_x[row] = masked(value, row) if row >= 10 else value
            value = (ry + down(ry, edge)) * (
                0.5 / (sigma + load("sy", row) + (four_y_band if row == BAND else four_y_main))
            )
            value = masked(value, row) if row == BAND else value
            if row == BAND:
                psi_x["y"] = value
            t.store("py", row, value + up(value, edge))
            value = (rz + load("rz", row, -1)) * (0.5 / (sigma + load("sg", row, -1) + four_z))
            t.store("sz", row, value)

        def potential(row):
            p1 = t.get("p1")
            sigma = load("sg", row)
            flux_x[row] = sigma * (next_x(p1, row) - p1(row))
            if row < 2:
                return
            edge = edges.get(("p1", row))
            flux_z = sigma * (load("p1", row, 1) - p1(row))
            t.store("fl", row, flux_z)
            flux_y = sigma * (up(p1(row), edge) - p1(row))
            if row == BAND:
                flux_x["y"] = flux_y
            total = (
                (prior_x(lambda r: flux_x[r], row) - flux_x[row])
                + (down(flux_y, edge) - flux_y)
                + (load("fl", row, -1) - flux_z)
            )
            value = p1(row) + load("rn", row) * (load("nr", row) - total)
            t.store("p2", row, masked(value, row) if row >= 10 else value)

        for step in (faces, residual, vector, potential):
            step(BAND)
        t.store("px", BAND, psi_x[BAND] + next_x(lambda r: psi_x[r], BAND))
        pairs = {
            "fx": pair(roll(load("fx", BAND), -3), roll(load("gz", BAND), 3)),
            "fz": pair(roll(load("fz", BAND), -3), roll(load("gx", BAND), 3)),
            "sy": pair(roll(psi_x["y"], -3), roll(load("ry", BAND), 3)),
            "p1": pair(roll(load("p1", BAND), -3), roll(flux_x["y"], 3)),
        }
        for row in range(0, 11):
            for name, both in pairs.items():
                edges[(name, row)] = border(both, row)
            faces(row)
            residual(row)
            if row >= 1:
                vector(row)
                potential(row)
            if row >= 2:
                t.store("px", row - 1, psi_x[row - 1] + psi_x[row])

    def pass_c(j):
        z0 = pl.multiple_of(j * TILE, TILE)
        t = Tile(z0)
        load = t.load
        zs = pl.ds(z0, TILE)
        edges = {}

        def half(row):
            t.store("pz", row, load("sz", row) + load("sz", row, 1))

        def faces(row):
            px, py, pz = load("px", row), load("py", row), load("pz", row)
            outer = row < 2 or row == BAND
            face = px - up(px, edges.get(("px", row))) + next_x(t.get("py"), row) - py
            t.store("qz", row, masked(face, row) if outer else face)
            face = pz - next_x(t.get("pz"), row) + load("px", row, 1) - px
            t.store("qy", row, masked(face, row) if outer else face)
            if row >= 2:
                face = py - load("py", row, 1) + up(pz, edges.get(("pz", row))) - pz
                t.store("qx", row, masked(face, row) if row == BAND else face)

        def finish(row):
            p2 = t.get("p2")
            sigma = load("sg", row)
            mid = p2(row)
            step = (
                next_x(p2, row) - mid + load("px", row),
                up(mid, edges[("p2", row)]) - mid + load("py", row),
                load("p2", row, 1) - mid + load("pz", row),
            )
            qx, qy, qz = load("qx", row), load("qy", row), load("qz", row)
            curl = (
                qz - down(qz, edges[("px", row)]) - qy + load("qy", row, -1),
                prior_x(t.get("qz"), row) - qz + qx - load("qx", row, -1),
                down(qx, edges[("pz", row)]) - qx + qy - prior_x(t.get("qy"), row),
            )
            for f, d in enumerate("xyz"):
                corr_out[row - 2, f, zs, :] = load("f" + d, row) + step[f]
                res_out[row - 2, f, zs, :] = load("r" + d, row) - curl[f] - sigma * step[f]

        half(BAND)
        faces(BAND)
        pairs = {
            "px": pair(roll(load("px", BAND), -3), roll(load("qz", BAND), 3)),
            "pz": pair(roll(load("pz", BAND), -3), roll(load("qx", BAND), 3)),
            "p2": roll(load("p2", BAND), -3),
        }
        half(1)
        for row in range(1, 10):
            for name, both in pairs.items():
                edges[(name, row)] = border(both, row)
            half(row + 1)
            faces(row)
            if row >= 2:
                finish(row)

    wait_bulk(0)
    pass_a(0)
    wait_bulk(1)
    pass_a(1)
    pass_b(0)

    def sweep(j, carry):
        wait_bulk(j)
        pass_a(j)
        pass_b(j - 1)
        pass_c(j - 2)
        return carry

    lax.fori_loop(2, tiles, sweep, 0)
    pass_b(tiles - 1)
    pass_c(tiles - 2)
    pass_c(tiles - 1)

    for side in range(2):

        @pl.when(x_there[side])
        def _():
            pair_of = pl.ds(2 * side, 2)
            wait_bytes(halo_rs.at[pair_of], x_send.at[side, 0])
            wait_bytes(halo_mat.at[pair_of], x_send.at[side, 1])

        @pl.when(y_there[side])
        def _():
            side_copy(side).wait_send()

    for q in range(4):

        @pl.when(c_there[q])
        def _():
            corner_copy(q).wait_send()


def leave(corr, res, corr_out, res_out, sem):
    copies = [
        pltpu.make_async_copy(source.at[x], target.at[:, :, x, :], sem.at[k])
        for x in range(corr.shape[0])
        for k, (source, target) in enumerate(((corr, corr_out), (res, res_out)))
    ]
    for copy in copies:
        copy.start()
    for k, source in enumerate((corr, res)):
        pltpu.make_async_copy(source, source, sem.at[k]).wait()


def solution(mesh):
    count_x, count_y = mesh.shape["gx"], mesh.shape["gy"]

    def local(right_side, material, conductivity):
        depth, rows, cols = material.shape
        f32 = jnp.float32
        dma = pltpu.SemaphoreType.DMA
        vmem = pl.BlockSpec(memory_space=pltpu.VMEM)
        hbm = pl.BlockSpec(memory_space=pltpu.HBM)
        tiles = depth // TILE
        made = jax.ShapeDtypeStruct((rows, 3, depth, cols), f32)
        corrected, final = pl.pallas_call(
            functools.partial(kernel, (count_x, count_y, depth, rows, cols)),
            out_shape=(made, made),
            in_specs=[hbm] * 3,
            out_specs=(vmem, vmem),
            scratch_shapes=[
                pltpu.SMEM((16,), f32),
                pltpu.VMEM((rows, 3, depth, cols), f32),
                pltpu.VMEM((rows, depth, cols), jnp.int32),
                pltpu.VMEM((4, 3, depth, cols), f32),
                pltpu.VMEM((4, depth, cols), jnp.int32),
                pltpu.VMEM((4, depth, LANES), f32),
                pltpu.VMEM((depth, LANES), f32),
                pltpu.VMEM((2, depth, LANES), f32),
                pltpu.VMEM((4, TILE, LANES), f32),
                pltpu.VMEM((4, TILE, LANES), f32),
            ]
            + [pltpu.VMEM((ROWS + 1, depth + 2 * PAD, LANES), f32)] * len(NAMES)
            + [
                dma((3,)),
                dma((2, 2)),
                dma((tiles, 2, 2)),
                dma((2,)),
                dma((2,)),
                dma((4,)),
                dma((4,)),
            ],
            compiler_params=pltpu.CompilerParams(
                collective_id=0, has_side_effects=True, vmem_limit_bytes=40 << 20
            ),
        )(
            *(
                pltpu.with_memory_space_constraint(value, pltpu.HBM)
                for value in (conductivity, right_side, material)
            )
        )
        out = jax.ShapeDtypeStruct(right_side.shape, f32)
        return pl.pallas_call(
            leave,
            out_shape=(out, out),
            in_specs=[vmem, vmem],
            out_specs=(hbm, hbm),
            scratch_shapes=[dma((2,))],
            compiler_params=pltpu.CompilerParams(vmem_limit_bytes=1 << 20),
        )(corrected, final)

    return jax.shard_map(
        local,
        mesh=mesh,
        in_specs=(P(None, None, "gx", "gy"), P(None, "gx", "gy"), P()),
        out_specs=(P(None, None, "gx", "gy"), P(None, None, "gx", "gy")),
        check_vma=False,
    )
```

time: 27.7 us -> 25.7 us (0.928)
  the two profiles are of different devices: /device:TPU:1 before, /device:TPU:24 now
where the time goes in v3:
time: 25.7 us; the launch traced here: 25.6 us
  Pallas kernels  24.9 us (97%)
  between operations  0.64 us (2%)
    pallas_call x1, Pallas kernels, local(): pl.pallas_call(functools.partial(kernel, (count_x, count_y, depth, rows,...  23.8 us
    pallas_call x1, Pallas kernels, local(): pl.pallas_call(leave, out_shape=(out, out), in_specs=[vmem, vmem], out_sp...  1.14 us

profile of v3, /device:TPU:24, one launch (start us, length us, event | category | flops | bytes accessed | tf_op | source)
XLA Modules:
  0.0 25.6 jit_solution(9884947205408446852)
XLA Ops:
  0.6 23.8 %shard_map.50 = (f32[8,3,64,128]{3,2,1,0:T(8,128)S(1)}, f32[8,3,64,128]{3,2,1,0:T(8,128)S(1)}) custom-call(f32[16]{0:T(128)} %cond_hbm.1, f32[3,64,8,128]{3,2,1,0:T(8,128)} %rs_hbm.1, s32[64,8,128]{2,1,0:T(8,128)} %mat_hbm.1), custom_call_target="tpu_custom_call" | custom-call | tf_op jit(solution)/shard_map/pallas_call | solution.py:610
  24.4 1.1 %shard_map.51 = (f32[3,64,8,128]{3,2,1,0:T(8,128)}, f32[3,64,8,128]{3,2,1,0:T(8,128)}) custom-call(f32[8,3,64,128]{3,2,1,0:T(8,128)S(1)} %get-tuple-element.4.corr, f32[8,3,64,128]{3,2,1,0:T(8,128)S(1)} %get-tuple-element.5.res), custom_call_target="tpu_custom_call" | custom-call | tf_op jit(solution)/shard_map/pallas_call | solution.py:647

commit v4 on v3

--- a/solution.py
+++ b/solution.py
@@ -16,6 +16,8 @@
 BAND = 12
 GROUP = 8
 EARLY = 3
+TOGETHER = 4
+WIDTH = 2
 MESH = pl.DeviceIdType.MESH
 
 NAMES = (
@@ -34,6 +36,12 @@
 
 def turn(value, shift):
     return pltpu.roll(value, lax.rem(shift + 2 * LANES, LANES), 1)
+
+
+def together(steps):
+    steps = list(steps)
+    while steps:
+        steps = [one for one in steps if next(one, "end") is None]
 
 
 def kernel(
@@ -211,7 +219,7 @@
         wait_bytes(raw, in_sem.at[0])
         table = class_table()
 
-        def prepare(j, carry):
+        def prepare(j):
             z0 = pl.multiple_of(j * TILE, TILE)
             zs = pl.ds(z0, TILE)
             packed = [zeros] * 4
@@ -220,21 +228,25 @@
                 values.append(look_up(table, mat[x, zs, :]))
                 start_row(x + 2, values, pl.ds(PAD + z0, TILE))
                 packed = ends(values, x + 2, packed)
-            up, down = zeros, zeros
+                yield
+            north, south = zeros, zeros
             for f in range(4):
                 pack[f, zs, :] = packed[f]
                 mine = place // 2 == f
-                up = jnp.where(mine, roll(packed[f], 2 * f - 2), up)
-                down = jnp.where(mine, roll(packed[f], 2 * f - 4), down)
-            side_msg[zs, :] = jnp.where((lane >= 16) & (lane < 80), up, roll(down, 64))
+                north = jnp.where(mine, roll(packed[f], 2 * f - 2), north)
+                south = jnp.where(mine, roll(packed[f], 2 * f - 4), south)
+            both = jnp.where((lane >= 16) & (lane < 80), north, roll(south, 64))
+            side_msg[zs, :] = both
+
+        def several(g, carry):
+            together(prepare(g * TOGETHER + k) for k in range(TOGETHER))
             return carry
 
-        lax.fori_loop(0, tiles, prepare, 0)
+        lax.fori_loop(0, tiles // TOGETHER, several, 0)
         for q, start in enumerate((64, 0, 16, 80)):
             value = zeros
             for k in range(tiles):
-                source = side_msg[TILE * k : TILE * (k + 1), :]
-                value = jnp.where(lane // 16 == k, roll(source, 16 * k - start), value)
+                value = jnp.where(lane // 16 == k, roll(side_msg[TILE * k : TILE * (k + 1), :], 16 * k - start), value)
             corner[q] = value
         for row in range(ROWS + 1):
             for name in READ_BELOW:
@@ -264,10 +276,18 @@
 
     period = max(count_x // 2, 2)
     early = lax.rem(ix, period) < period // 2
-    pl.when(early)(prepare_all)
-    pl.semaphore_wait(barrier, expected)
-    send_bulk(0, EARLY)
-    pl.when(~early)(prepare_all)
+
+    def begin(turn_of, carry):
+        pl.when(early == (turn_of == 0))(prepare_all)
+
+        @pl.when(turn_of == 0)
+        def _():
+            pl.semaphore_wait(barrier, expected)
+            send_bulk(0, EARLY)
+
+        return carry
+
+    lax.fori_loop(0, 2, begin, 0)
     for q in range(4):
 
         @pl.when(c_there[q])
@@ -359,6 +379,7 @@
             values.append(look_up(table, halo_mat[slot, zs, :]))
             start_row(row, values, there)
             packed = ends(values, row, packed)
+        yield
         low = jnp.where(lane < 80, side_recv[0, zs, :], turn(corner_recv[2], 80 - 16 * j))
         low = jnp.where(lane < 16, turn(corner_recv[0], -16 * j), low)
         high = jnp.where(
@@ -374,6 +395,7 @@
             for f in range(4)
         ]
         start_row(BAND, values, there)
+        yield
         sg, tx = t.get("sg"), t.get("tx")
         both = pair(roll(t.load("ty", BAND), 2), roll(sg(BAND), 3))
         for row in [BAND] + list(range(1, 12)):
@@ -394,6 +416,7 @@
             t.store("p1", row, weight * total)
             t.store("rn", row, weight)
             t.store("nr", row, total)
+            yield
 
     def pass_b(j):
         z0 = pl.multiple_of(j * TILE, TILE)
@@ -473,6 +496,7 @@
 
         for step in (faces, residual, vector, potential):
             step(BAND)
+            yield
         t.store("px", BAND, psi_x[BAND] + next_x(lambda r: psi_x[r], BAND))
         pairs = {
             "fx": pair(roll(load("fx", BAND), -3), roll(load("gz", BAND), 3)),
@@ -490,6 +514,7 @@
                 potential(row)
             if row >= 2:
                 t.store("px", row - 1, psi_x[row - 1] + psi_x[row])
+            yield
 
     def pass_c(j):
         z0 = pl.multiple_of(j * TILE, TILE)
@@ -533,6 +558,7 @@
 
         half(BAND)
         faces(BAND)
+        yield
         pairs = {
             "px": pair(roll(load("px", BAND), -3), roll(load("qz", BAND), 3)),
             "pz": pair(roll(load("pz", BAND), -3), roll(load("qx", BAND), 3)),
@@ -546,24 +572,31 @@
             faces(row)
             if row >= 2:
                 finish(row)
-
-    wait_bulk(0)
-    pass_a(0)
-    wait_bulk(1)
-    pass_a(1)
-    pass_b(0)
-
-    def sweep(j, carry):
-        wait_bulk(j)
-        pass_a(j)
-        pass_b(j - 1)
-        pass_c(j - 2)
+            yield
+
+    groups = tiles // WIDTH
+
+    def sweep(g, carry):
+        def over(one, group):
+            together(one(group * WIDTH + k) for k in range(WIDTH))
+
+        @pl.when(g < groups)
+        def _():
+            for k in range(WIDTH):
+                wait_bulk(g * WIDTH + k)
+            over(pass_a, g)
+
+        @pl.when((g >= 1) & (g < groups + 1))
+        def _():
+            over(pass_b, g - 1)
+
+        @pl.when(g >= 2)
+        def _():
+            over(pass_c, g - 2)
+
         return carry
 
-    lax.fori_loop(2, tiles, sweep, 0)
-    pass_b(tiles - 1)
-    pass_c(tiles - 2)
-    pass_c(tiles - 1)
+    lax.fori_loop(0, groups + 2, sweep, 0)
 
     for side in range(2):
 

time: 25.7 us -> 23.1 us (0.90)
  Pallas kernels: 24.9 us -> 22.4 us
    pallas_call x1, Pallas kernels: 23.8 us -> 21.2 us  [local(): pl.pallas_call(functools.partial(kernel, (count_x, count_y, depth, rows,...]
where the time goes in v4:
time: 23.1 us; the launch traced here: 23 us
  Pallas kernels  22.4 us (97%)
  between operations  0.64 us (3%)
    pallas_call x1, Pallas kernels, local(): pl.pallas_call(functools.partial(kernel, (count_x, count_y, depth, rows,...  21.2 us
    pallas_call x1, Pallas kernels, local(): pl.pallas_call(leave, out_shape=(out, out), in_specs=[vmem, vmem], out_sp...  1.14 us

profile of v4, /device:TPU:24, one launch (start us, length us, event | category | flops | bytes accessed | tf_op | source)
XLA Modules:
  0.0 23.0 jit_solution(491009962300429023)
XLA Ops:
  0.6 21.2 %shard_map.50 = (f32[8,3,64,128]{3,2,1,0:T(8,128)S(1)}, f32[8,3,64,128]{3,2,1,0:T(8,128)S(1)}) custom-call(f32[16]{0:T(128)} %cond_hbm.1, f32[3,64,8,128]{3,2,1,0:T(8,128)} %rs_hbm.1, s32[64,8,128]{2,1,0:T(8,128)} %mat_hbm.1), custom_call_target="tpu_custom_call" | custom-call | tf_op jit(solution)/shard_map/pallas_call | solution.py:643
  21.9 1.1 %shard_map.51 = (f32[3,64,8,128]{3,2,1,0:T(8,128)}, f32[3,64,8,128]{3,2,1,0:T(8,128)}) custom-call(f32[8,3,64,128]{3,2,1,0:T(8,128)S(1)} %get-tuple-element.4.corr, f32[8,3,64,128]{3,2,1,0:T(8,128)S(1)} %get-tuple-element.5.res), custom_call_target="tpu_custom_call" | custom-call | tf_op jit(solution)/shard_map/pallas_call | solution.py:680

commit v5 on v4

--- a/solution.py
+++ b/solution.py
@@ -13,11 +13,13 @@
 TILE = 8
 PAD = 8
 ROWS = 12
-BAND = 12
+LOW, HIGH = 12, 13
+BANDS = (LOW, HIGH)
 GROUP = 8
 EARLY = 3
 TOGETHER = 4
 WIDTH = 2
+BAND_TILES = 4
 MESH = pl.DeviceIdType.MESH
 
 NAMES = (
@@ -117,10 +119,9 @@
         def _():
             corner_recv[q] = zeros
 
-    def bulk(side, z0):
-        zs = pl.ds(z0, TILE)
+    def bulk(side, j):
+        zs = pl.ds(pl.multiple_of(j * TILE, TILE), TILE)
         first_row = (rows - 2, 0)[side]
-        j = z0 // TILE
         copies = []
         for k in range(2):
             slot = 2 * side + k
@@ -145,9 +146,12 @@
 
             @pl.when(x_there[side])
             def _():
-                for j in range(start, stop):
-                    for copy in bulk(side, j * TILE):
+                def send(j, carry):
+                    for copy in bulk(side, j):
                         copy.start()
+                    return carry
+
+                lax.fori_loop(start, stop, send, 0)
 
     def wait_bytes(ref, sem):
         pltpu.make_async_copy(ref, ref, sem).wait()
@@ -168,13 +172,15 @@
     row_of = lane // GROUP
     to_f32 = lambda flag: jnp.where(flag, 1.0, 0.0).astype(jnp.float32)
     inside_x = ((row_of >= 2) | low_x) & ((row_of < 10) | high_x)
-    inside_y = ((place >= 2) | low_y) & ((place < 6) | high_y)
-    band_mask = to_f32(inside_x & inside_y)
+    band_mask = {
+        LOW: to_f32(inside_x & ((place >= 2) | low_y)),
+        HIGH: to_f32(inside_x & ((place < 6) | high_y)),
+    }
     mask_low, mask_high = to_f32(low_x), to_f32(high_x)
 
     def mask_of(row):
-        if row == BAND:
-            return band_mask
+        if row in BANDS:
+            return band_mask[row]
         if row < 2:
             return mask_low
         if row >= 10:
@@ -198,10 +204,13 @@
         return level[0]
 
     def ends(values, row, packed):
-        chosen = (lane >= GROUP * row + 2) & (lane < GROUP * row + 6)
-        return [
-            jnp.where(chosen, roll(v, GROUP * row + 4), p) for v, p in zip(values, packed)
-        ]
+        lows, highs = packed
+        at = lane - GROUP * row
+        in_low, in_high = (at >= 2) & (at < 8), (at >= 0) & (at < 6)
+        return (
+            [jnp.where(in_low, roll(v, GROUP * row + 2), p) for v, p in zip(values, lows)],
+            [jnp.where(in_high, roll(v, GROUP * row + 6), p) for v, p in zip(values, highs)],
+        )
 
     def start_row(row, values, there, keep_sigma=True):
         sigma = masked(values[3], row)
@@ -222,7 +231,7 @@
         def prepare(j):
             z0 = pl.multiple_of(j * TILE, TILE)
             zs = pl.ds(z0, TILE)
-            packed = [zeros] * 4
+            packed = ([zeros] * 4, [zeros] * 4)
             for x in range(rows):
                 values = [raw[x, f, zs, :] for f in range(3)]
                 values.append(look_up(table, mat[x, zs, :]))
@@ -231,10 +240,11 @@
                 yield
             north, south = zeros, zeros
             for f in range(4):
-                pack[f, zs, :] = packed[f]
+                for k in range(2):
+                    pack[k, f, zs, :] = packed[k][f]
                 mine = place // 2 == f
-                north = jnp.where(mine, roll(packed[f], 2 * f - 2), north)
-                south = jnp.where(mine, roll(packed[f], 2 * f - 4), south)
+                north = jnp.where(mine, roll(packed[1][f], 2 * f - 4), north)
+                south = jnp.where(mine, roll(packed[0][f], 2 * f - 2), south)
             both = jnp.where((lane >= 16) & (lane < 80), north, roll(south, 64))
             side_msg[zs, :] = both
 
@@ -248,7 +258,7 @@
             for k in range(tiles):
                 value = jnp.where(lane // 16 == k, roll(side_msg[TILE * k : TILE * (k + 1), :], 16 * k - start), value)
             corner[q] = value
-        for row in range(ROWS + 1):
+        for row in range(ROWS + 2):
             for name in READ_BELOW:
                 bufs[name][row, 0:PAD, :] = zeros
             for name in READ_ABOVE:
@@ -302,18 +312,6 @@
 
     send_bulk(EARLY, tiles)
     table = class_table()
-    for q in range(4):
-
-        @pl.when(c_there[3 - q])
-        def _():
-            corner_copy(q).wait_recv()
-
-    for side in range(2):
-
-        @pl.when(y_there[1 - side])
-        def _():
-            side_copy(side).wait_recv()
-
     class Tile:
         def __init__(self, z0):
             self.z0 = z0
@@ -332,119 +330,113 @@
         def get(self, name):
             return functools.partial(self.load, name)
 
-    def pair(first, second):
-        return jnp.where(place == 3, first, second)
-
-    def border(both, row):
-        return None if row == BAND else roll(both, LANES - 1 - (GROUP * row + 3))
-
-    def up(value, edge):
-        value = roll(value, -1)
-        return value if edge is None else jnp.where(lane == LANES - 1, edge, value)
-
-    def down(value, edge):
-        value = roll(value, 1)
-        return value if edge is None else jnp.where(lane == 0, edge, value)
-
-    def down_early(value, edge):
-        if edge is not None:
-            value = jnp.where(lane == LANES - 1, edge, value)
+    def up(value):
+        return roll(value, -1)
+
+    def down(value):
         return roll(value, 1)
 
     def next_x(get, row):
-        return roll(get(BAND), -GROUP) if row == BAND else get(row + 1)
+        return roll(get(row), -GROUP) if row in BANDS else get(row + 1)
 
     def prior_x(get, row):
-        return roll(get(BAND), GROUP) if row == BAND else get(row - 1)
-
-    four_x_band = 4.0 + 4.0 * roll(band_mask, GROUP)
-    four_y_band = 4.0 + 4.0 * roll(band_mask, 1)
-    four_y_main = jnp.where((lane == 0) & ~low_y, 4.0, 8.0)
+        return roll(get(row), GROUP) if row in BANDS else get(row - 1)
+
+    four_x_band = {row: 4.0 + 4.0 * roll(band_mask[row], GROUP) for row in BANDS}
+    four_y_band = {row: 4.0 + 4.0 * roll(band_mask[row], 1) for row in BANDS}
 
     def four_x(row):
-        if row == BAND:
-            return four_x_band
+        if row in BANDS:
+            return four_x_band[row]
         mask = mask_of(row - 1)
         return 8.0 if mask is None else 4.0 + 4.0 * mask
+
+    def four_y(row):
+        return four_y_band[row] if row in BANDS else 8.0
+
+    def nodal(t, row):
+        sg, tx, ty = t.get("sg"), t.get("tx"), t.load("ty", row)
+        sigma_y = down(sg(row))
+        t.store("sy", row, sigma_y)
+        total = (
+            (prior_x(tx, row) - tx(row))
+            + (down(ty) - ty)
+            + (t.load("tz", row, -1) - t.load("tz", row))
+        )
+        weight = 3.0 * sg(row) + prior_x(sg, row) + sigma_y + t.load("sg", row, -1)
+        mask = mask_of(row)
+        if mask is not None:
+            weight = weight + (1.0 - mask)
+        weight = masked(OMEGA_NODE / weight, row)
+        t.store("p1", row, weight * total)
+        t.store("rn", row, weight)
+        t.store("nr", row, total)
 
     def pass_a(j):
         z0 = pl.multiple_of(j * TILE, TILE)
         t = Tile(z0)
         zs = pl.ds(z0, TILE)
-        there = pl.ds(PAD + z0, TILE)
-        packed = [pack[f, zs, :] for f in range(4)]
         for row in (0, 1, 10, 11):
             slot = row if row < 2 else row - 8
             values = [halo_rs[slot, f, zs, :] for f in range(3)]
             values.append(look_up(table, halo_mat[slot, zs, :]))
-            start_row(row, values, there)
+            start_row(row, values, pl.ds(PAD + z0, TILE))
+            yield
+        for row in range(1, 12):
+            nodal(t, row)
+            yield
+
+    def band_a(j):
+        z0 = pl.multiple_of(j * TILE, TILE)
+        t = Tile(z0)
+        zs = pl.ds(z0, TILE)
+        packed = tuple([pack[k, f, zs, :] for f in range(4)] for k in range(2))
+        for row in (0, 1, 10, 11):
+            slot = row if row < 2 else row - 8
+            values = [halo_rs[slot, f, zs, :] for f in range(3)] + [t.load("sg", row)]
             packed = ends(values, row, packed)
-        yield
+            yield
         low = jnp.where(lane < 80, side_recv[0, zs, :], turn(corner_recv[2], 80 - 16 * j))
         low = jnp.where(lane < 16, turn(corner_recv[0], -16 * j), low)
         high = jnp.where(
             lane < 80, roll(side_recv[1, zs, :], 64), turn(corner_recv[3], 80 - 16 * j)
         )
         high = jnp.where(lane < 16, turn(corner_recv[1], -16 * j), high)
+        yield
+        values = [jnp.where(place < 2, roll(low, -2 * f), packed[0][f]) for f in range(4)]
+        start_row(LOW, values, pl.ds(PAD + z0, TILE))
         values = [
-            jnp.where(
-                place < 4,
-                jnp.where(place < 2, roll(low, -2 * f), roll(packed[f], -2)),
-                jnp.where(place < 6, roll(packed[f], 2), roll(high, 6 - 2 * f)),
-            )
-            for f in range(4)
+            jnp.where(place < 6, packed[1][f], roll(high, 6 - 2 * f)) for f in range(4)
         ]
-        start_row(BAND, values, there)
+        start_row(HIGH, values, pl.ds(PAD + z0, TILE))
         yield
-        sg, tx = t.get("sg"), t.get("tx")
-        both = pair(roll(t.load("ty", BAND), 2), roll(sg(BAND), 3))
-        for row in [BAND] + list(range(1, 12)):
-            edge = border(both, row)
-            sigma_y = down(sg(row), edge)
-            t.store("sy", row, sigma_y)
-            ty = t.load("ty", row)
-            total = (
-                (prior_x(tx, row) - tx(row))
-                + (down_early(ty, edge) - ty)
-                + (t.load("tz", row, -1) - t.load("tz", row))
-            )
-            nodal = 3.0 * sg(row) + prior_x(sg, row) + sigma_y + t.load("sg", row, -1)
-            mask = mask_of(row)
-            if mask is not None:
-                nodal = nodal + (1.0 - mask)
-            weight = masked(OMEGA_NODE / nodal, row)
-            t.store("p1", row, weight * total)
-            t.store("rn", row, weight)
-            t.store("nr", row, total)
+        for row in BANDS:
+            nodal(t, row)
             yield
 
-    def pass_b(j):
-        z0 = pl.multiple_of(j * TILE, TILE)
-        t = Tile(z0)
-        load = t.load
-        four_z = jnp.where((sub == 0) & (j == 0), 4.0, 8.0)
-        edges = {}
-        psi_x, flux_x = {}, {}
-
-        def faces(row):
+    class Middle:
+        def __init__(self, j):
+            self.t = Tile(pl.multiple_of(j * TILE, TILE))
+            self.psi_x, self.flux_x = {}, {}
+            self.four_z = jnp.where((sub == 0) & (j == 0), 4.0, 8.0)
+
+        def faces(self, row):
+            t, load = self.t, self.t.load
             fx, fy, fz = load("fx", row), load("fy", row), load("fz", row)
-            outer = row < 2 or row == BAND
-            edge = edges.get(("fx", row))
-            face = fx - up(fx, edge) + next_x(t.get("fy"), row) - fy
+            outer = row < 2 or row in BANDS
+            face = fx - up(fx) + next_x(t.get("fy"), row) - fy
             t.store("gz", row, masked(face, row) if outer else face)
             face = fz - next_x(t.get("fz"), row) + load("fx", row, 1) - fx
             t.store("gy", row, masked(face, row) if outer else face)
             if row >= 1:
-                edge = edges.get(("fz", row))
-                face = fy - load("fy", row, 1) + up(fz, edge) - fz
+                face = fy - load("fy", row, 1) + up(fz) - fz
                 t.store("gx", row, masked(face, row) if outer else face)
 
-        def residual(row):
+        def residual(self, row):
+            t, load = self.t, self.t.load
             gz, gy = load("gz", row), load("gy", row)
-            value = load("tx", row) - (
-                gz - down(gz, edges.get(("fx", row))) - gy + load("gy", row, -1)
-            )
-            t.store("rx", row, masked(value, row) if row == BAND else value)
+            value = load("tx", row) - (gz - down(gz) - gy + load("gy", row, -1))
+            t.store("rx", row, masked(value, row) if row in BANDS else value)
             if row >= 1:
                 gx = load("gx", row)
                 value = load("ty", row) - (
@@ -452,127 +444,138 @@
                 )
                 t.store("ry", row, masked(value, row) if row >= 10 else value)
                 value = load("tz", row) - (
-                    down(gx, edges.get(("fz", row))) - gx + gy - prior_x(t.get("gy"), row)
+                    down(gx) - gx + gy - prior_x(t.get("gy"), row)
                 )
                 t.store("rz", row, masked(value, row) if row >= 10 else value)
 
-        def vector(row):
+        def vector(self, row):
+            t, load = self.t, self.t.load
             sigma = load("sg", row)
             rx, ry, rz = load("rx", row), load("ry", row), load("rz", row)
-            edge = edges.get(("sy", row))
             value = (rx + prior_x(t.get("rx"), row)) * (
                 0.5 / (sigma + prior_x(t.get("sg"), row) + four_x(row))
             )
-            psi_x[row] = masked(value, row) if row >= 10 else value
-            value = (ry + down(ry, edge)) * (
-                0.5 / (sigma + load("sy", row) + (four_y_band if row == BAND else four_y_main))
+            self.psi_x[row] = masked(value, row) if row >= 10 else value
+            value = (ry + down(ry)) * (0.5 / (sigma + load("sy", row) + four_y(row)))
+            value = masked(value, row) if row in BANDS else value
+            t.store("py", row, value + up(value))
+            value = (rz + load("rz", row, -1)) * (
+                0.5 / (sigma + load("sg", row, -1) + self.four_z)
             )
-            value = masked(value, row) if row == BAND else value
-            if row == BAND:
-                psi_x["y"] = value
-            t.store("py", row, value + up(value, edge))
-            value = (rz + load("rz", row, -1)) * (0.5 / (sigma + load("sg", row, -1) + four_z))
             t.store("sz", row, value)
 
-        def potential(row):
+        def potential(self, row):
+            t, load, flux = self.t, self.t.load, self.flux_x
             p1 = t.get("p1")
             sigma = load("sg", row)
-            flux_x[row] = sigma * (next_x(p1, row) - p1(row))
+            flux[row] = sigma * (next_x(p1, row) - p1(row))
             if row < 2:
                 return
-            edge = edges.get(("p1", row))
             flux_z = sigma * (load("p1", row, 1) - p1(row))
             t.store("fl", row, flux_z)
-            flux_y = sigma * (up(p1(row), edge) - p1(row))
-            if row == BAND:
-                flux_x["y"] = flux_y
+            flux_y = sigma * (up(p1(row)) - p1(row))
             total = (
-                (prior_x(lambda r: flux_x[r], row) - flux_x[row])
-                + (down(flux_y, edge) - flux_y)
+                (prior_x(lambda r: flux[r], row) - flux[row])
+                + (down(flux_y) - flux_y)
                 + (load("fl", row, -1) - flux_z)
             )
             value = p1(row) + load("rn", row) * (load("nr", row) - total)
             t.store("p2", row, masked(value, row) if row >= 10 else value)
 
-        for step in (faces, residual, vector, potential):
-            step(BAND)
+    def pass_b(j):
+        m = Middle(j)
+        for row in range(0, 11):
+            m.faces(row)
+            m.residual(row)
+            if row >= 1:
+                m.vector(row)
+                m.potential(row)
+            if row >= 2:
+                m.t.store("px", row - 1, m.psi_x[row - 1] + m.psi_x[row])
             yield
-        t.store("px", BAND, psi_x[BAND] + next_x(lambda r: psi_x[r], BAND))
-        pairs = {
-            "fx": pair(roll(load("fx", BAND), -3), roll(load("gz", BAND), 3)),
-            "fz": pair(roll(load("fz", BAND), -3), roll(load("gx", BAND), 3)),
-            "sy": pair(roll(psi_x["y"], -3), roll(load("ry", BAND), 3)),
-            "p1": pair(roll(load("p1", BAND), -3), roll(flux_x["y"], 3)),
-        }
-        for row in range(0, 11):
-            for name, both in pairs.items():
-                edges[(name, row)] = border(both, row)
-            faces(row)
-            residual(row)
-            if row >= 1:
-                vector(row)
-                potential(row)
-            if row >= 2:
-                t.store("px", row - 1, psi_x[row - 1] + psi_x[row])
-            yield
-
-    def pass_c(j):
-        z0 = pl.multiple_of(j * TILE, TILE)
-        t = Tile(z0)
-        load = t.load
-        zs = pl.ds(z0, TILE)
-        edges = {}
-
-        def half(row):
-            t.store("pz", row, load("sz", row) + load("sz", row, 1))
-
-        def faces(row):
+
+    def band_b(j):
+        m = Middle(j)
+        for step in (m.faces, m.residual, m.vector, m.potential):
+            for row in BANDS:
+                step(row)
+                yield
+        for row in BANDS:
+            m.t.store("px", row, m.psi_x[row] + next_x(lambda r: m.psi_x[r], row))
+
+    class Last:
+        def __init__(self, j):
+            self.z0 = pl.multiple_of(j * TILE, TILE)
+            self.t = Tile(self.z0)
+
+        def half(self, row):
+            load = self.t.load
+            self.t.store("pz", row, load("sz", row) + load("sz", row, 1))
+
+        def faces(self, row):
+            t, load = self.t, self.t.load
             px, py, pz = load("px", row), load("py", row), load("pz", row)
-            outer = row < 2 or row == BAND
-            face = px - up(px, edges.get(("px", row))) + next_x(t.get("py"), row) - py
+            outer = row < 2 or row in BANDS
+            face = px - up(px) + next_x(t.get("py"), row) - py
             t.store("qz", row, masked(face, row) if outer else face)
             face = pz - next_x(t.get("pz"), row) + load("px", row, 1) - px
             t.store("qy", row, masked(face, row) if outer else face)
             if row >= 2:
-                face = py - load("py", row, 1) + up(pz, edges.get(("pz", row))) - pz
-                t.store("qx", row, masked(face, row) if row == BAND else face)
-
-        def finish(row):
+                face = py - load("py", row, 1) + up(pz) - pz
+                t.store("qx", row, masked(face, row) if row in BANDS else face)
+
+        def finish(self, row):
+            t, load = self.t, self.t.load
             p2 = t.get("p2")
             sigma = load("sg", row)
             mid = p2(row)
             step = (
                 next_x(p2, row) - mid + load("px", row),
-                up(mid, edges[("p2", row)]) - mid + load("py", row),
+                up(mid) - mid + load("py", row),
                 load("p2", row, 1) - mid + load("pz", row),
             )
             qx, qy, qz = load("qx", row), load("qy", row), load("qz", row)
             curl = (
-                qz - down(qz, edges[("px", row)]) - qy + load("qy", row, -1),
+                qz - down(qz) - qy + load("qy", row, -1),
                 prior_x(t.get("qz"), row) - qz + qx - load("qx", row, -1),
-                down(qx, edges[("pz", row)]) - qx + qy - prior_x(t.get("qy"), row),
+                down(qx) - qx + qy - prior_x(t.get("qy"), row),
             )
-            for f, d in enumerate("xyz"):
-                corr_out[row - 2, f, zs, :] = load("f" + d, row) + step[f]
-                res_out[row - 2, f, zs, :] = load("r" + d, row) - curl[f] - sigma * step[f]
-
-        half(BAND)
-        faces(BAND)
+            return [
+                (load("f" + d, row) + step[f], load("r" + d, row) - curl[f] - sigma * step[f])
+                for f, d in enumerate("xyz")
+            ]
+
+    def pass_c(j):
+        m = Last(j)
+        m.half(1)
+        for row in range(1, 10):
+            m.half(row + 1)
+            m.faces(row)
+            if row >= 2:
+                for f, values in enumerate(m.finish(row)):
+                    for out, value in zip((corr_out, res_out), values):
+                        out[row - 2, f, pl.ds(m.z0, TILE), :] = value
+            yield
+
+    def band_c(j):
+        m = Last(j)
+        zs = pl.ds(m.z0, TILE)
+        for step in (m.half, m.faces):
+            for row in BANDS:
+                step(row)
+            yield
+        lows, highs = m.finish(LOW), m.finish(HIGH)
         yield
-        pairs = {
-            "px": pair(roll(load("px", BAND), -3), roll(load("qz", BAND), 3)),
-            "pz": pair(roll(load("pz", BAND), -3), roll(load("qx", BAND), 3)),
-            "p2": roll(load("p2", BAND), -3),
-        }
-        half(1)
-        for row in range(1, 10):
-            for name, both in pairs.items():
-                edges[(name, row)] = border(both, row)
-            half(row + 1)
-            faces(row)
-            if row >= 2:
-                finish(row)
-            yield
+        at_end = (lane < 2) | (lane >= LANES - 2)
+        for f in range(3):
+            for k, out in enumerate((corr_out, res_out)):
+                both = jnp.where(place < 6, highs[f][k], roll(lows[f][k], 4))
+                for row in range(2, 10):
+                    edge = roll(both, LANES - 6 - GROUP * row)
+                    out[row - 2, f, zs, :] = jnp.where(
+                        at_end, edge, out[row - 2, f, zs, :]
+                    )
+                yield
 
     groups = tiles // WIDTH
 
@@ -597,6 +600,26 @@
         return carry
 
     lax.fori_loop(0, groups + 2, sweep, 0)
+
+    for q in range(4):
+
+        @pl.when(c_there[3 - q])
+        def _():
+            corner_copy(q).wait_recv()
+
+    for side in range(2):
+
+        @pl.when(y_there[1 - side])
+        def _():
+            side_copy(side).wait_recv()
+
+    for one in (band_a, band_b, band_c):
+
+        def over_bands(g, carry):
+            together(one(g * BAND_TILES + k) for k in range(BAND_TILES))
+            return carry
+
+        lax.fori_loop(0, tiles // BAND_TILES, over_bands, 0)
 
     for side in range(2):
 
@@ -651,13 +674,13 @@
                 pltpu.VMEM((rows, depth, cols), jnp.int32),
                 pltpu.VMEM((4, 3, depth, cols), f32),
                 pltpu.VMEM((4, depth, cols), jnp.int32),
-                pltpu.VMEM((4, depth, LANES), f32),
+                pltpu.VMEM((2, 4, depth, LANES), f32),
                 pltpu.VMEM((depth, LANES), f32),
                 pltpu.VMEM((2, depth, LANES), f32),
                 pltpu.VMEM((4, TILE, LANES), f32),
                 pltpu.VMEM((4, TILE, LANES), f32),
             ]
-            + [pltpu.VMEM((ROWS + 1, depth + 2 * PAD, LANES), f32)] * len(NAMES)
+            + [pltpu.VMEM((ROWS + 2, depth + 2 * PAD, LANES), f32)] * len(NAMES)
             + [
                 dma((3,)),
                 dma((2, 2)),

time: 23.1 us -> 22.3 us (0.965)
  Pallas kernels: 22.4 us -> 21.6 us
    pallas_call x1, Pallas kernels: 21.2 us -> 20.4 us  [local(): pl.pallas_call(functools.partial(kernel, (count_x, count_y, depth, rows,...]
where the time goes in v5:
time: 22.3 us; the launch traced here: 22.2 us
  Pallas kernels  21.6 us (97%)
  between operations  0.64 us (3%)
    pallas_call x1, Pallas kernels, local(): pl.pallas_call(functools.partial(kernel, (count_x, count_y, depth, rows,...  20.4 us
    pallas_call x1, Pallas kernels, local(): pl.pallas_call(leave, out_shape=(out, out), in_specs=[vmem, vmem], out_sp...  1.14 us

profile of v5, /device:TPU:24, one launch (start us, length us, event | category | flops | bytes accessed | tf_op | source)
XLA Modules:
  0.0 22.2 jit_solution(5420935204823773361)
XLA Ops:
  0.6 20.4 %shard_map.50 = (f32[8,3,64,128]{3,2,1,0:T(8,128)S(1)}, f32[8,3,64,128]{3,2,1,0:T(8,128)S(1)}) custom-call(f32[16]{0:T(128)} %cond_hbm.1, f32[3,64,8,128]{3,2,1,0:T(8,128)} %rs_hbm.1, s32[64,8,128]{2,1,0:T(8,128)} %mat_hbm.1), custom_call_target="tpu_custom_call" | custom-call | tf_op jit(solution)/shard_map/pallas_call | solution.py:666
  21.1 1.1 %shard_map.51 = (f32[3,64,8,128]{3,2,1,0:T(8,128)}, f32[3,64,8,128]{3,2,1,0:T(8,128)}) custom-call(f32[8,3,64,128]{3,2,1,0:T(8,128)S(1)} %get-tuple-element.4.corr, f32[8,3,64,128]{3,2,1,0:T(8,128)S(1)} %get-tuple-element.5.res), custom_call_target="tpu_custom_call" | custom-call | tf_op jit(solution)/shard_map/pallas_call | solution.py:703

commit v6 on v5

--- a/solution.py
+++ b/solution.py
@@ -16,7 +16,6 @@
 LOW, HIGH = 12, 13
 BANDS = (LOW, HIGH)
 GROUP = 8
-EARLY = 3
 TOGETHER = 4
 WIDTH = 2
 BAND_TILES = 4
@@ -84,11 +83,6 @@
     )
     c_there = (high_x & high_y, high_x & low_y, low_x & high_y, low_x & low_y)
 
-    pltpu.make_async_copy(cond_hbm, cond, in_sem.at[2]).start()
-    for x in range(rows):
-        pltpu.make_async_copy(mat_hbm.at[:, x, :], mat.at[x], in_sem.at[1]).start()
-        pltpu.make_async_copy(rs_hbm.at[:, :, x, :], raw.at[x], in_sem.at[0]).start()
-
     barrier = pltpu.get_barrier_semaphore()
     expected = 0
     for there, present in zip(
@@ -223,6 +217,10 @@
         bufs["sg"][row, there, :] = sigma
 
     def prepare_all():
+        pltpu.make_async_copy(cond_hbm, cond, in_sem.at[2]).start()
+        for x in range(rows):
+            pltpu.make_async_copy(mat_hbm.at[:, x, :], mat.at[x], in_sem.at[1]).start()
+            pltpu.make_async_copy(rs_hbm.at[:, :, x, :], raw.at[x], in_sem.at[0]).start()
         pltpu.make_async_copy(cond_hbm, cond, in_sem.at[2]).wait()
         wait_bytes(mat, in_sem.at[1])
         wait_bytes(raw, in_sem.at[0])
@@ -293,7 +291,7 @@
         @pl.when(turn_of == 0)
         def _():
             pl.semaphore_wait(barrier, expected)
-            send_bulk(0, EARLY)
+            send_bulk(0, tiles)
 
         return carry
 
@@ -310,7 +308,6 @@
         def _():
             side_copy(side).start()
 
-    send_bulk(EARLY, tiles)
     table = class_table()
     class Tile:
         def __init__(self, z0):

time: 22.3 us -> 22.2 us (level)
  no operation moved by 1% of the time
where the time goes in v6:
time: 22.2 us; the launch traced here: 22.1 us
  Pallas kernels  21.5 us (97%)
  between operations  0.64 us (3%)
    pallas_call x1, Pallas kernels, local(): pl.pallas_call(functools.partial(kernel, (count_x, count_y, depth, rows,...  20.3 us
    pallas_call x1, Pallas kernels, local(): pl.pallas_call(leave, out_shape=(out, out), in_specs=[vmem, vmem], out_sp...  1.14 us

profile of v6, /device:TPU:24, one launch (start us, length us, event | category | flops | bytes accessed | tf_op | source)
XLA Modules:
  0.0 22.1 jit_solution(10464793082533923047)
XLA Ops:
  0.6 20.3 %shard_map.50 = (f32[8,3,64,128]{3,2,1,0:T(8,128)S(1)}, f32[8,3,64,128]{3,2,1,0:T(8,128)S(1)}) custom-call(f32[16]{0:T(128)} %cond_hbm.1, f32[3,64,8,128]{3,2,1,0:T(8,128)} %rs_hbm.1, s32[64,8,128]{2,1,0:T(8,128)} %mat_hbm.1), custom_call_target="tpu_custom_call" | custom-call | tf_op jit(solution)/shard_map/pallas_call | solution.py:663
  21.0 1.1 %shard_map.51 = (f32[3,64,8,128]{3,2,1,0:T(8,128)}, f32[3,64,8,128]{3,2,1,0:T(8,128)}) custom-call(f32[8,3,64,128]{3,2,1,0:T(8,128)S(1)} %get-tuple-element.4.corr, f32[8,3,64,128]{3,2,1,0:T(8,128)S(1)} %get-tuple-element.5.res), custom_call_target="tpu_custom_call" | custom-call | tf_op jit(solution)/shard_map/pallas_call | solution.py:700

commit v7 on v6

--- a/solution.py
+++ b/solution.py
@@ -18,7 +18,6 @@
 GROUP = 8
 TOGETHER = 4
 WIDTH = 2
-BAND_TILES = 4
 MESH = pl.DeviceIdType.MESH
 
 NAMES = (
@@ -610,13 +609,13 @@
         def _():
             side_copy(side).wait_recv()
 
-    for one in (band_a, band_b, band_c):
+    for one, size in ((band_a, 8), (band_b, 4), (band_c, 2)):
 
         def over_bands(g, carry):
-            together(one(g * BAND_TILES + k) for k in range(BAND_TILES))
+            together(one(g * size + k) for k in range(size))
             return carry
 
-        lax.fori_loop(0, tiles // BAND_TILES, over_bands, 0)
+        lax.fori_loop(0, tiles // size, over_bands, 0)
 
     for side in range(2):
 

time: 22.2 us -> 21.9 us (0.986)
  Pallas kernels: 21.5 us -> 21.2 us
    pallas_call x1, Pallas kernels: 20.3 us -> 20 us  [local(): pl.pallas_call(functools.partial(kernel, (count_x, count_y, depth, rows,...]
where the time goes in v7:
time: 21.9 us; the launch traced here: 21.8 us
  Pallas kernels  21.2 us (97%)
  between operations  0.64 us (3%)
    pallas_call x1, Pallas kernels, local(): pl.pallas_call(functools.partial(kernel, (count_x, count_y, depth, rows,...  20 us
    pallas_call x1, Pallas kernels, local(): pl.pallas_call(leave, out_shape=(out, out), in_specs=[vmem, vmem], out_sp...  1.14 us

profile of v7, /device:TPU:24, one launch (start us, length us, event | category | flops | bytes accessed | tf_op | source)
XLA Modules:
  0.0 21.8 jit_solution(13683323685099465943)
XLA Ops:
  0.6 20.0 %shard_map.50 = (f32[8,3,64,128]{3,2,1,0:T(8,128)S(1)}, f32[8,3,64,128]{3,2,1,0:T(8,128)S(1)}) custom-call(f32[16]{0:T(128)} %cond_hbm.1, f32[3,64,8,128]{3,2,1,0:T(8,128)} %rs_hbm.1, s32[64,8,128]{2,1,0:T(8,128)} %mat_hbm.1), custom_call_target="tpu_custom_call" | custom-call | tf_op jit(solution)/shard_map/pallas_call | solution.py:662
  20.7 1.1 %shard_map.51 = (f32[3,64,8,128]{3,2,1,0:T(8,128)}, f32[3,64,8,128]{3,2,1,0:T(8,128)}) custom-call(f32[8,3,64,128]{3,2,1,0:T(8,128)S(1)} %get-tuple-element.4.corr, f32[8,3,64,128]{3,2,1,0:T(8,128)S(1)} %get-tuple-element.5.res), custom_call_target="tpu_custom_call" | custom-call | tf_op jit(solution)/shard_map/pallas_call | solution.py:699

commit v8 on v7

--- a/solution.py
+++ b/solution.py
@@ -16,7 +16,7 @@
 LOW, HIGH = 12, 13
 BANDS = (LOW, HIGH)
 GROUP = 8
-TOGETHER = 4
+TOGETHER = 8
 WIDTH = 2
 MESH = pl.DeviceIdType.MESH
 

time: 21.9 us -> 21.9 us (level)
  no operation moved by 1% of the time
where the time goes in v8:
time: 21.9 us; the launch traced here: 21.8 us
  Pallas kernels  21.2 us (97%)
  between operations  0.64 us (3%)
    pallas_call x1, Pallas kernels, local(): pl.pallas_call(functools.partial(kernel, (count_x, count_y, depth, rows,...  20 us
    pallas_call x1, Pallas kernels, local(): pl.pallas_call(leave, out_shape=(out, out), in_specs=[vmem, vmem], out_sp...  1.14 us

profile of v8, /device:TPU:24, one launch (start us, length us, event | category | flops | bytes accessed | tf_op | source)
XLA Modules:
  0.0 21.8 jit_solution(5456106194091379390)
XLA Ops:
  0.6 20.0 %shard_map.50 = (f32[8,3,64,128]{3,2,1,0:T(8,128)S(1)}, f32[8,3,64,128]{3,2,1,0:T(8,128)S(1)}) custom-call(f32[16]{0:T(128)} %cond_hbm.1, f32[3,64,8,128]{3,2,1,0:T(8,128)} %rs_hbm.1, s32[64,8,128]{2,1,0:T(8,128)} %mat_hbm.1), custom_call_target="tpu_custom_call" | custom-call | tf_op jit(solution)/shard_map/pallas_call | solution.py:662
  20.7 1.1 %shard_map.51 = (f32[3,64,8,128]{3,2,1,0:T(8,128)}, f32[3,64,8,128]{3,2,1,0:T(8,128)}) custom-call(f32[8,3,64,128]{3,2,1,0:T(8,128)S(1)} %get-tuple-element.4.corr, f32[8,3,64,128]{3,2,1,0:T(8,128)S(1)} %get-tuple-element.5.res), custom_call_target="tpu_custom_call" | custom-call | tf_op jit(solution)/shard_map/pallas_call | solution.py:699
